TPU v7x, 1024 devices: a whole 4x8x16 slice. The times are simulated.
1024 devices in a mesh: dp: 32 (over y, x), section: 16 (over z), group: 2 (over core).
Axes of the slice: x: 4, y: 8, z: 16, core: 2. Of those that a mesh axis runs over, the one named last changes fastest.
Arguments:
- tokens_in: bfloat16 [8192, 4096], P(('dp', 'group')), may hold values from -6 to 6
- cotangent: bfloat16 [8192, 4096], P(('dp', 'group')), may hold values from -6 to 6
- gains: float32 [16, 4096], P('section'), may hold values from 0.5 to 1.5
- w_qkv: bfloat16 [16, 4096, 384], P('section'), may hold values from -0.09375 to 0.09375
- w_out: bfloat16 [16, 128, 4096], P('section'), may hold values from -0.5 to 0.5
- segments: int32 [512, 16], P(('dp', 'group')), may hold values from 0 to 3, never falling along the last dimension, each value on 1 to 8 neighbouring positions
- plan: int32 [64, 8], P(('dp', 'group')), may hold values from 0 to 7, each once within a row
Outputs:
- input_grads: bfloat16 [16, 8192, 4096], P('section', ('dp', 'group'))
- gain_grads: float32 [16, 4096], P('section')
Inputs may be any that keep to these rules, and one draw needn't show every extreme that they name: Each row of plan names every one of 0 .. 7 once. `segments`: segment numbers never fall along a row and every episode lies within one row.
All inputs are finite; a program needn't handle non-finite values.
Results may differ from a plain program's by a relative error of at most 0.029.
Values may be sent and summed in bfloat16 or wider, within the bound.
A program may use at most 32 MiB of HBM per device.

v0:
```python
import math

import jax
import jax.numpy as jnp
from jax import lax
from jax.sharding import PartitionSpec as P

MB_ROWS = 2


def in_one_piece(arrays, axis, split_dim, concat_dim, along):
    widths = [math.prod(a.shape[along:]) for a in arrays]
    both = jnp.concatenate(
        [a.reshape(*a.shape[:along], w) for a, w in zip(arrays, widths)], axis=along
    )
    out = lax.all_to_all(both, axis, split_axis=split_dim, concat_axis=concat_dim, tiled=True)
    tiles = jnp.split(out, [sum(widths[:k]) for k in range(1, len(widths))], axis=along)
    return tuple((b.reshape(*out.shape[:along], *a.shape[along:]) for a, b in zip(arrays, tiles)))


def passed_along(array, axis, by):
    devices = lax.axis_size(axis)
    pairs = [(i, i + by) for i in range(devices) if 0 <= i + by < devices]
    return lax.ppermute(array, axis, pairs)


def sent_to_all(array, axis):
    copies = jnp.broadcast_to(array, (lax.axis_size(axis), *array.shape))
    return lax.all_to_all(copies, axis, split_axis=0, concat_axis=0, tiled=True)


def of_everyone(array, axis):
    everything = sent_to_all(array, axis)
    return jnp.sum(everything, axis=0)


def attend(hidden, segment, gain_row, w_layer, out_layer):
    count = hidden.shape[0]
    length = hidden.shape[1]
    width = hidden.shape[2]
    head = out_layer.shape[0]
    scaled = (
        hidden * lax.rsqrt(jnp.mean(hidden * hidden, axis=-1, keepdims=True) + 1e-05) * gain_row
    )
    normed = scaled.astype(jnp.bfloat16).reshape(count * length, width)
    projected = jnp.dot(normed, w_layer, preferred_element_type=jnp.float32).reshape(
        count, length, 3 * head
    )
    query = projected[:, :, :head]
    keyed = projected[:, :, head : 2 * head]
    valued = projected[:, :, 2 * head :]
    positions = jnp.arange(length)
    allowed = (positions[:, None] >= positions[None, :])[None] & (
        segment[:, :, None] == segment[:, None, :]
    )
    scores = jnp.einsum("rid,rjd->rij", query, keyed, precision=lax.Precision.HIGHEST) / math.sqrt(
        head
    )
    scores = jnp.where(allowed, scores, -1e30)
    weights = jax.nn.softmax(scores, axis=-1)
    mixed = jnp.einsum("rij,rjd->rid", weights, valued, precision=lax.Precision.HIGHEST)
    mixed = mixed.astype(jnp.bfloat16).reshape(count * length, head)
    output = jnp.dot(mixed, out_layer, preferred_element_type=jnp.float32).reshape(
        count, length, width
    )
    return hidden + output


def local(tokens_in, cotangent, gains, w_qkv, w_out, segments, plan):
    sections = lax.axis_size("section")
    section_index = lax.axis_index("section")
    rows_dev = plan.shape[1]
    width = tokens_in.shape[1]
    row_len = segments.shape[1]
    micro = rows_dev // MB_ROWS
    blocks = tokens_in.reshape(rows_dev, row_len, width)
    chosen = jnp.take(blocks, plan[0], axis=0)
    chosen_seg = jnp.take(segments, plan[0], axis=0).astype(jnp.bfloat16)
    assigned, moved_seg = in_one_piece((chosen, chosen_seg), "group", 0, 0, 2)
    assigned = assigned.reshape(micro, MB_ROWS, row_len, width)
    seg_groups = moved_seg.reshape(micro, MB_ROWS, row_len)
    gain_row = gains[0]
    w_layer = w_qkv[0]
    out_layer = w_out[0]
    grad_rows = cotangent.reshape(micro, MB_ROWS, row_len, width)
    ticks = micro + sections - 1

    def forward_tick(tick, carry):
        saved, arrived = carry
        index = tick - section_index
        valid = (index >= 0) & (index < micro)
        clipped = jnp.clip(index, 0, micro - 1)
        first_in = lax.dynamic_index_in_dim(assigned, clipped, 0, keepdims=False)
        entering = jnp.where(section_index == 0, first_in, arrived)
        kept = lax.dynamic_index_in_dim(saved, clipped, 0, keepdims=False)
        saved = lax.dynamic_update_index_in_dim(saved, jnp.where(valid, entering, kept), clipped, 0)
        segment = lax.dynamic_index_in_dim(seg_groups, clipped, 0, keepdims=False)

        def run_layer(value):
            return attend(value.astype(jnp.float32), segment, gain_row, w_layer, out_layer).astype(
                jnp.bfloat16
            )

        def skip_layer(value):
            return jnp.zeros_like(value)

        leaving = lax.cond(valid, run_layer, skip_layer, entering)
        arrived = passed_along(leaving, "section", 1)
        return (saved, arrived)

    saved_init = jnp.zeros((micro, MB_ROWS, row_len, width), jnp.bfloat16)
    arrive_init = jnp.zeros((MB_ROWS, row_len, width), jnp.bfloat16)
    saved, _ = lax.fori_loop(0, ticks, forward_tick, (saved_init, arrive_init))

    def backward_tick(tick, carry):
        grads_x, gain_total, arrived = carry
        index = tick - (sections - 1 - section_index)
        valid = (index >= 0) & (index < micro)
        clipped = jnp.clip(index, 0, micro - 1)
        last_in = lax.dynamic_index_in_dim(grad_rows, clipped, 0, keepdims=False)
        entering = jnp.where(section_index == sections - 1, last_in, arrived)
        segment = lax.dynamic_index_in_dim(seg_groups, clipped, 0, keepdims=False)
        stored = lax.dynamic_index_in_dim(saved, clipped, 0, keepdims=False).astype(jnp.float32)

        def local_layer(hidden, gains_here):
            return attend(hidden, segment, gains_here, w_layer, out_layer)

        def run_back(value):
            _, pullback = jax.vjp(local_layer, stored, gain_row)
            grad_hidden, grad_gain = pullback(value.astype(jnp.float32))
            return (grad_hidden.astype(jnp.bfloat16), grad_gain)

        def skip_back(value):
            return (jnp.zeros_like(value), jnp.zeros(gain_row.shape, jnp.float32))

        sending, grad_gain = lax.cond(valid, run_back, skip_back, entering)
        kept = lax.dynamic_index_in_dim(grads_x, clipped, 0, keepdims=False)
        grads_x = lax.dynamic_update_index_in_dim(
            grads_x, jnp.where(valid, sending, kept), clipped, 0
        )
        gain_total = gain_total + grad_gain
        arrived = passed_along(sending, "section", -1)
        return (grads_x, gain_total, arrived)

    grads_init = jnp.zeros((micro, MB_ROWS, row_len, width), jnp.bfloat16)
    gain_init = jnp.zeros(gain_row.shape, jnp.float32)
    grads_x, gain_total, _ = lax.fori_loop(
        0, ticks, backward_tick, (grads_init, gain_init, arrive_init)
    )
    gain_whole = of_everyone(gain_total, ("dp", "group"))
    return (grads_x.reshape(1, rows_dev * row_len, width), gain_whole[None])


def solution(mesh):
    placed = (
        P(("dp", "group"), None),
        P(("dp", "group"), None),
        P("section", None),
        P("section", None, None),
        P("section", None, None),
        P(("dp", "group"), None),
        P(("dp", "group"), None),
    )
    return jax.shard_map(
        local,
        mesh=mesh,
        in_specs=placed,
        out_specs=(P("section", ("dp", "group"), None), P("section", None)),
        check_vma=False,
    )
```

profile of v0, /device:TPU:1, one launch (start us, length us, event | category | flops | bytes accessed | tf_op | source)
XLA Modules:
  0.0 627.6 jit_solution(17884859737381781878)
XLA Ops:
  5.4 17.8 %all-to-all-start = ((bf16[8,16,4097]{2,1,0:T(8,128)(2,1)}), bf16[8,16,4097]{2,1,0:T(8,128)(2,1)S(1)}, u32[]{:S(2)}, u32[]{:S(2)}) async-start(bf16[8,16,4097]{2,1,0:T(8,128)(2,1)} %pad_maximum_fusion), calls=%async_computation | async-start | bytes 2162688 | tf_op jit(solution)/shard_map/all_to_all | solution.py:16
  27.0 237.9 %while.36 = (s32[]{:T(128)}, bf16[4,2,16,4096]{3,2,1,0:T(8,128)(2,1)S(1)}, bf16[2,16,4096]{2,1,0:T(8,128)(2,1)}, s32[]{:T(128)}, pred[]{:T(512)}, /*index=5*/bf1...) while((s32[]{:T(128)}, ...), condition=%wide.region_6.7_spmd, body=%wide.region_0.6_spmd.sunk | while | flops 137373408 | bytes 9333325 | solution.py:113
  28.1 4.1 conditional.5
  33.5 5.8 collective-permute-done
  49.4 5.0 collective-permute-done
  64.4 4.1 collective-permute-done
  84.6 7.2 %collective-permute-start = (bf16[2,16,4096]{2,1,0:T(8,128)(2,1)}, bf16[2,16,4096]{2,1,0:T(8,128)(2,1)S(1)}, u32[]{:S(2)}, u32[]{:S(2)}) collective-permute-start(bf16[2,16,4096]{2,1,0:T(8,128)(2,1)} %get-tuple-element.927), channel_id=1, source_target_pairs={{0,2},{2,4},{4,6},{6,8},{8,10},{10,12},{12,14},{14,16},{16,18},{18... | collective-permute-start | bytes 786440 | tf_op jit(solution)/shard_map/while/body/eval_jaxpr/ppermute | solution.py:24
  107.8 5.9 collective-permute-start
  129.8 7.1 %collective-permute-start = (bf16[2,16,4096]{2,1,0:T(8,128)(2,1)}, bf16[2,16,4096]{2,1,0:T(8,128)(2,1)S(1)}, u32[]{:S(2)}, u32[]{:S(2)}) collective-permute-start(bf16[2,16,4096]{2,1,0:T(8,128)(2,1)} %get-tuple-element.927), channel_id=1, source_target_pairs={{0,2},{2,4},{4,6},{6,8},{8,10},{10,12},{12,14},{14,16},{16,18},{18... | collective-permute-start | bytes 786440 | tf_op jit(solution)/shard_map/while/body/eval_jaxpr/ppermute | solution.py:24
  143.1 5.0 collective-permute-start
  154.2 8.4 %collective-permute-start = (bf16[2,16,4096]{2,1,0:T(8,128)(2,1)}, bf16[2,16,4096]{2,1,0:T(8,128)(2,1)S(1)}, u32[]{:S(2)}, u32[]{:S(2)}) collective-permute-start(bf16[2,16,4096]{2,1,0:T(8,128)(2,1)} %get-tuple-element.927), channel_id=1, source_target_pairs={{0,2},{2,4},{4,6},{6,8},{8,10},{10,12},{12,14},{14,16},{16,18},{18... | collective-permute-start | bytes 786440 | tf_op jit(solution)/shard_map/while/body/eval_jaxpr/ppermute | solution.py:24
  168.7 5.0 collective-permute-start
  173.7 4.4 collective-permute-done
  180.7 5.6 collective-permute-start
  186.3 5.6 collective-permute-done
  194.4 5.9 collective-permute-start
  200.3 6.1 collective-permute-done
  208.9 5.3 collective-permute-start
  214.2 4.9 collective-permute-done
  221.6 4.6 collective-permute-start
  232.5 5.3 collective-permute-start
  243.9 5.3 collective-permute-start
  255.3 5.3 collective-permute-start
  266.7 290.0 %while.37 = (s32[]{:T(128)}, bf16[4,2,16,4096]{3,2,1,0:T(8,128)(2,1)}, f32[4096]{0:T(1024)S(1)}, bf16[2,16,4096]{2,1,0:T(8,128)(2,1)}, s32[]{:T(128)}, /*index=5...) while((s32[]{:T(128)}, ...), condition=%wide.region_16.17_spmd.clone, body=%wide.region_7.16_spmd.clone.sunk | while | flops 242546624 | bytes 26482452 | solution.py:147
  269.8 6.0 collective-permute-done.1
  278.9 5.7 collective-permute-done.1
  287.7 8.4 %collective-permute-done.1 = bf16[2,16,4096]{2,1,0:T(8,128)(2,1)} collective-permute-done((bf16[2,16,4096]{2,1,0:T(8,128)(2,1)S(1)}, bf16[2,16,4096]{2,1,0:T(8,128)(2,1)}, u32[]{:S(2)}, u32[]{:S(2)}) %collective-permute-start.1) | collective-permute-done | bytes 262176 | tf_op jit(solution)/shard_map/while/body/eval_jaxpr/ppermute | solution.py:24
  299.3 7.3 %collective-permute-done.1 = bf16[2,16,4096]{2,1,0:T(8,128)(2,1)} collective-permute-done((bf16[2,16,4096]{2,1,0:T(8,128)(2,1)S(1)}, bf16[2,16,4096]{2,1,0:T(8,128)(2,1)}, u32[]{:S(2)}, u32[]{:S(2)}) %collective-permute-start.1) | collective-permute-done | bytes 262176 | tf_op jit(solution)/shard_map/while/body/eval_jaxpr/ppermute | solution.py:24
  309.6 4.9 collective-permute-done.1
  317.6 4.2 collective-permute-done.1
  324.9 4.2 collective-permute-done.1
  332.1 11.2 %collective-permute-done.1 = bf16[2,16,4096]{2,1,0:T(8,128)(2,1)} collective-permute-done((bf16[2,16,4096]{2,1,0:T(8,128)(2,1)S(1)}, bf16[2,16,4096]{2,1,0:T(8,128)(2,1)}, u32[]{:S(2)}, u32[]{:S(2)}) %collective-permute-start.1) | collective-permute-done | bytes 262176 | tf_op jit(solution)/shard_map/while/body/eval_jaxpr/ppermute | solution.py:24
  346.5 5.3 collective-permute-done.1
  354.9 4.9 collective-permute-done.1
  362.9 5.4 collective-permute-done.1
  371.4 6.5 %collective-permute-done.1 = bf16[2,16,4096]{2,1,0:T(8,128)(2,1)} collective-permute-done((bf16[2,16,4096]{2,1,0:T(8,128)(2,1)S(1)}, bf16[2,16,4096]{2,1,0:T(8,128)(2,1)}, u32[]{:S(2)}, u32[]{:S(2)}) %collective-permute-start.1) | collective-permute-done | bytes 262176 | tf_op jit(solution)/shard_map/while/body/eval_jaxpr/ppermute | solution.py:24
  381.0 8.1 %collective-permute-done.1 = bf16[2,16,4096]{2,1,0:T(8,128)(2,1)} collective-permute-done((bf16[2,16,4096]{2,1,0:T(8,128)(2,1)S(1)}, bf16[2,16,4096]{2,1,0:T(8,128)(2,1)}, u32[]{:S(2)}, u32[]{:S(2)}) %collective-permute-start.1) | collective-permute-done | bytes 262176 | tf_op jit(solution)/shard_map/while/body/eval_jaxpr/ppermute | solution.py:24
  392.2 8.8 %collective-permute-done.1 = bf16[2,16,4096]{2,1,0:T(8,128)(2,1)} collective-permute-done((bf16[2,16,4096]{2,1,0:T(8,128)(2,1)S(1)}, bf16[2,16,4096]{2,1,0:T(8,128)(2,1)}, u32[]{:S(2)}, u32[]{:S(2)}) %collective-permute-start.1) | collective-permute-done | bytes 262176 | tf_op jit(solution)/shard_map/while/body/eval_jaxpr/ppermute | solution.py:24
  404.1 86.8 %collective-permute-done.1 = bf16[2,16,4096]{2,1,0:T(8,128)(2,1)} collective-permute-done((bf16[2,16,4096]{2,1,0:T(8,128)(2,1)S(1)}, bf16[2,16,4096]{2,1,0:T(8,128)(2,1)}, u32[]{:S(2)}, u32[]{:S(2)}) %collective-permute-start.1) | collective-permute-done | bytes 262176 | tf_op jit(solution)/shard_map/while/body/eval_jaxpr/ppermute | solution.py:24
  490.9 7.0 %conditional.6 = (bf16[2,16,4096]{2,1,0:T(8,128)(2,1)S(1)}, f32[4096]{0:T(1024)S(1)}) conditional(s32[]{:T(128)} %convert_element_type.119, () %tuple.107, (pred[]{:T(512)}, bf16[4,2,16,4096]{3,2,1,0:T(8,128)(2,1)}, s32[]{:T(128)}, bf16[2,16,4096]{2,1,0:T(8,128)(2,1)}, bf16[4,2,16]{2,1,0:T(2,128)(2,1)S(1)}, ...), branch_computations={%region_8.8_spmd, %region_9.15_spmd} | conditional | flops 242407360 | bytes 24073156 | solution.py:136
  500.9 5.4 collective-permute-done.1
  506.3 7.0 %conditional.6 = (bf16[2,16,4096]{2,1,0:T(8,128)(2,1)S(1)}, f32[4096]{0:T(1024)S(1)}) conditional(s32[]{:T(128)} %convert_element_type.119, () %tuple.107, (pred[]{:T(512)}, bf16[4,2,16,4096]{3,2,1,0:T(8,128)(2,1)}, s32[]{:T(128)}, bf16[2,16,4096]{2,1,0:T(8,128)(2,1)}, bf16[4,2,16]{2,1,0:T(2,128)(2,1)S(1)}, ...), branch_computations={%region_8.8_spmd, %region_9.15_spmd} | conditional | flops 242407360 | bytes 24073156 | solution.py:136
  516.3 6.8 %collective-permute-done.1 = bf16[2,16,4096]{2,1,0:T(8,128)(2,1)} collective-permute-done((bf16[2,16,4096]{2,1,0:T(8,128)(2,1)S(1)}, bf16[2,16,4096]{2,1,0:T(8,128)(2,1)}, u32[]{:S(2)}, u32[]{:S(2)}) %collective-permute-start.1) | collective-permute-done | bytes 262176 | tf_op jit(solution)/shard_map/while/body/eval_jaxpr/ppermute | solution.py:24
  523.2 7.0 %conditional.6 = (bf16[2,16,4096]{2,1,0:T(8,128)(2,1)S(1)}, f32[4096]{0:T(1024)S(1)}) conditional(s32[]{:T(128)} %convert_element_type.119, () %tuple.107, (pred[]{:T(512)}, bf16[4,2,16,4096]{3,2,1,0:T(8,128)(2,1)}, s32[]{:T(128)}, bf16[2,16,4096]{2,1,0:T(8,128)(2,1)}, bf16[4,2,16]{2,1,0:T(2,128)(2,1)S(1)}, ...), branch_computations={%region_8.8_spmd, %region_9.15_spmd} | conditional | flops 242407360 | bytes 24073156 | solution.py:136
  533.2 8.3 %collective-permute-done.1 = bf16[2,16,4096]{2,1,0:T(8,128)(2,1)} collective-permute-done((bf16[2,16,4096]{2,1,0:T(8,128)(2,1)S(1)}, bf16[2,16,4096]{2,1,0:T(8,128)(2,1)}, u32[]{:S(2)}, u32[]{:S(2)}) %collective-permute-start.1) | collective-permute-done | bytes 262176 | tf_op jit(solution)/shard_map/while/body/eval_jaxpr/ppermute | solution.py:24
  541.5 7.0 %conditional.6 = (bf16[2,16,4096]{2,1,0:T(8,128)(2,1)S(1)}, f32[4096]{0:T(1024)S(1)}) conditional(s32[]{:T(128)} %convert_element_type.119, () %tuple.107, (pred[]{:T(512)}, bf16[4,2,16,4096]{3,2,1,0:T(8,128)(2,1)}, s32[]{:T(128)}, bf16[2,16,4096]{2,1,0:T(8,128)(2,1)}, bf16[4,2,16]{2,1,0:T(2,128)(2,1)S(1)}, ...), branch_computations={%region_8.8_spmd, %region_9.15_spmd} | conditional | flops 242407360 | bytes 24073156 | solution.py:136
  551.5 5.2 collective-permute-done.1
  557.7 68.3 %all_to_all.11 = f32[64,1,4096]{2,1,0:T(1,128)S(1)} all-to-all(f32[64,1,4096]{2,1,0:T(1,128)S(1)} %broadcast_in_dim.91), channel_id=1, replica_groups=mesh['dp'=32,'section'=16,'group'=2] {'dp','group'}, dimensions={0} | all-to-all | bytes 2097152 | tf_op jit(solution)/shard_map/all_to_all | solution.py:29
  (397 shorter events, 247.7 us)
Async XLA Ops:
  0.6 1.4 copy-start
  5.4 21.6 %copy-start.2 = (bf16[1,128,4096]{2,1,0:T(8,128)(2,1)S(1)}, bf16[1,128,4096]{2,1,0:T(8,128)(2,1)}, u32[]{:S(2)}) copy-start(bf16[1,128,4096]{2,1,0:T(8,128)(2,1)} %param.19) | copy-start | bytes 3145732
  5.4 21.6 %copy-start.3 = (f32[1,4096]{1,0:T(1,128)S(1)}, f32[1,4096]{1,0:T(1,128)}, u32[]{:S(2)}) copy-start(f32[1,4096]{1,0:T(1,128)} %param.17) | copy-start | bytes 49156
  5.4 19.6 %all-to-all-start = ((bf16[8,16,4097]{2,1,0:T(8,128)(2,1)}), bf16[8,16,4097]{2,1,0:T(8,128)(2,1)S(1)}, u32[]{:S(2)}, u32[]{:S(2)}) async-start(bf16[8,16,4097]{2,1,0:T(8,128)(2,1)} %pad_maximum_fusion), calls=%async_computation | async-start | bytes 2162688 | tf_op jit(solution)/shard_map/all_to_all | solution.py:16
  32.2 7.2 %collective-permute-start = (bf16[2,16,4096]{2,1,0:T(8,128)(2,1)}, bf16[2,16,4096]{2,1,0:T(8,128)(2,1)S(1)}, u32[]{:S(2)}, u32[]{:S(2)}) collective-permute-start(bf16[2,16,4096]{2,1,0:T(8,128)(2,1)} %get-tuple-element.927), channel_id=1, source_target_pairs={{0,2},{2,4},{4,6},{6,8},{8,10},{10,12},{12,14},{14,16},{16,18},{18... | collective-permute-start | bytes 786440 | tf_op jit(solution)/shard_map/while/body/eval_jaxpr/ppermute | solution.py:24
  39.4 0.7 copy-start.4
  45.3 9.1 %collective-permute-start = (bf16[2,16,4096]{2,1,0:T(8,128)(2,1)}, bf16[2,16,4096]{2,1,0:T(8,128)(2,1)S(1)}, u32[]{:S(2)}, u32[]{:S(2)}) collective-permute-start(bf16[2,16,4096]{2,1,0:T(8,128)(2,1)} %get-tuple-element.927), channel_id=1, source_target_pairs={{0,2},{2,4},{4,6},{6,8},{8,10},{10,12},{12,14},{14,16},{16,18},{18... | collective-permute-start | bytes 786440 | tf_op jit(solution)/shard_map/while/body/eval_jaxpr/ppermute | solution.py:24
  54.4 0.7 copy-start.4
  60.3 8.2 %collective-permute-start = (bf16[2,16,4096]{2,1,0:T(8,128)(2,1)}, bf16[2,16,4096]{2,1,0:T(8,128)(2,1)S(1)}, u32[]{:S(2)}, u32[]{:S(2)}) collective-permute-start(bf16[2,16,4096]{2,1,0:T(8,128)(2,1)} %get-tuple-element.927), channel_id=1, source_target_pairs={{0,2},{2,4},{4,6},{6,8},{8,10},{10,12},{12,14},{14,16},{16,18},{18... | collective-permute-start | bytes 786440 | tf_op jit(solution)/shard_map/while/body/eval_jaxpr/ppermute | solution.py:24
  74.4 7.7 %collective-permute-start = (bf16[2,16,4096]{2,1,0:T(8,128)(2,1)}, bf16[2,16,4096]{2,1,0:T(8,128)(2,1)S(1)}, u32[]{:S(2)}, u32[]{:S(2)}) collective-permute-start(bf16[2,16,4096]{2,1,0:T(8,128)(2,1)} %get-tuple-element.927), channel_id=1, source_target_pairs={{0,2},{2,4},{4,6},{6,8},{8,10},{10,12},{12,14},{14,16},{16,18},{18... | collective-permute-start | bytes 786440 | tf_op jit(solution)/shard_map/while/body/eval_jaxpr/ppermute | solution.py:24
  84.6 10.8 %collective-permute-start = (bf16[2,16,4096]{2,1,0:T(8,128)(2,1)}, bf16[2,16,4096]{2,1,0:T(8,128)(2,1)S(1)}, u32[]{:S(2)}, u32[]{:S(2)}) collective-permute-start(bf16[2,16,4096]{2,1,0:T(8,128)(2,1)} %get-tuple-element.927), channel_id=1, source_target_pairs={{0,2},{2,4},{4,6},{6,8},{8,10},{10,12},{12,14},{14,16},{16,18},{18... | collective-permute-start | bytes 786440 | tf_op jit(solution)/shard_map/while/body/eval_jaxpr/ppermute | solution.py:24
  97.9 7.4 %collective-permute-start = (bf16[2,16,4096]{2,1,0:T(8,128)(2,1)}, bf16[2,16,4096]{2,1,0:T(8,128)(2,1)S(1)}, u32[]{:S(2)}, u32[]{:S(2)}) collective-permute-start(bf16[2,16,4096]{2,1,0:T(8,128)(2,1)} %get-tuple-element.927), channel_id=1, source_target_pairs={{0,2},{2,4},{4,6},{6,8},{8,10},{10,12},{12,14},{14,16},{16,18},{18... | collective-permute-start | bytes 786440 | tf_op jit(solution)/shard_map/while/body/eval_jaxpr/ppermute | solution.py:24
  107.8 9.5 %collective-permute-start = (bf16[2,16,4096]{2,1,0:T(8,128)(2,1)}, bf16[2,16,4096]{2,1,0:T(8,128)(2,1)S(1)}, u32[]{:S(2)}, u32[]{:S(2)}) collective-permute-start(bf16[2,16,4096]{2,1,0:T(8,128)(2,1)} %get-tuple-element.927), channel_id=1, source_target_pairs={{0,2},{2,4},{4,6},{6,8},{8,10},{10,12},{12,14},{14,16},{16,18},{18... | collective-permute-start | bytes 786440 | tf_op jit(solution)/shard_map/while/body/eval_jaxpr/ppermute | solution.py:24
  119.9 7.4 %collective-permute-start = (bf16[2,16,4096]{2,1,0:T(8,128)(2,1)}, bf16[2,16,4096]{2,1,0:T(8,128)(2,1)S(1)}, u32[]{:S(2)}, u32[]{:S(2)}) collective-permute-start(bf16[2,16,4096]{2,1,0:T(8,128)(2,1)} %get-tuple-element.927), channel_id=1, source_target_pairs={{0,2},{2,4},{4,6},{6,8},{8,10},{10,12},{12,14},{14,16},{16,18},{18... | collective-permute-start | bytes 786440 | tf_op jit(solution)/shard_map/while/body/eval_jaxpr/ppermute | solution.py:24
  129.8 10.7 %collective-permute-start = (bf16[2,16,4096]{2,1,0:T(8,128)(2,1)}, bf16[2,16,4096]{2,1,0:T(8,128)(2,1)S(1)}, u32[]{:S(2)}, u32[]{:S(2)}) collective-permute-start(bf16[2,16,4096]{2,1,0:T(8,128)(2,1)} %get-tuple-element.927), channel_id=1, source_target_pairs={{0,2},{2,4},{4,6},{6,8},{8,10},{10,12},{12,14},{14,16},{16,18},{18... | collective-permute-start | bytes 786440 | tf_op jit(solution)/shard_map/while/body/eval_jaxpr/ppermute | solution.py:24
  143.1 8.6 %collective-permute-start = (bf16[2,16,4096]{2,1,0:T(8,128)(2,1)}, bf16[2,16,4096]{2,1,0:T(8,128)(2,1)S(1)}, u32[]{:S(2)}, u32[]{:S(2)}) collective-permute-start(bf16[2,16,4096]{2,1,0:T(8,128)(2,1)} %get-tuple-element.927), channel_id=1, source_target_pairs={{0,2},{2,4},{4,6},{6,8},{8,10},{10,12},{12,14},{14,16},{16,18},{18... | collective-permute-start | bytes 786440 | tf_op jit(solution)/shard_map/while/body/eval_jaxpr/ppermute | solution.py:24
  154.2 12.0 %collective-permute-start = (bf16[2,16,4096]{2,1,0:T(8,128)(2,1)}, bf16[2,16,4096]{2,1,0:T(8,128)(2,1)S(1)}, u32[]{:S(2)}, u32[]{:S(2)}) collective-permute-start(bf16[2,16,4096]{2,1,0:T(8,128)(2,1)} %get-tuple-element.927), channel_id=1, source_target_pairs={{0,2},{2,4},{4,6},{6,8},{8,10},{10,12},{12,14},{14,16},{16,18},{18... | collective-permute-start | bytes 786440 | tf_op jit(solution)/shard_map/while/body/eval_jaxpr/ppermute | solution.py:24
  168.7 9.4 %collective-permute-start = (bf16[2,16,4096]{2,1,0:T(8,128)(2,1)}, bf16[2,16,4096]{2,1,0:T(8,128)(2,1)S(1)}, u32[]{:S(2)}, u32[]{:S(2)}) collective-permute-start(bf16[2,16,4096]{2,1,0:T(8,128)(2,1)} %get-tuple-element.927), channel_id=1, source_target_pairs={{0,2},{2,4},{4,6},{6,8},{8,10},{10,12},{12,14},{14,16},{16,18},{18... | collective-permute-start | bytes 786440 | tf_op jit(solution)/shard_map/while/body/eval_jaxpr/ppermute | solution.py:24
  180.7 11.2 %collective-permute-start = (bf16[2,16,4096]{2,1,0:T(8,128)(2,1)}, bf16[2,16,4096]{2,1,0:T(8,128)(2,1)S(1)}, u32[]{:S(2)}, u32[]{:S(2)}) collective-permute-start(bf16[2,16,4096]{2,1,0:T(8,128)(2,1)} %get-tuple-element.927), channel_id=1, source_target_pairs={{0,2},{2,4},{4,6},{6,8},{8,10},{10,12},{12,14},{14,16},{16,18},{18... | collective-permute-start | bytes 786440 | tf_op jit(solution)/shard_map/while/body/eval_jaxpr/ppermute | solution.py:24
  194.4 12.0 %collective-permute-start = (bf16[2,16,4096]{2,1,0:T(8,128)(2,1)}, bf16[2,16,4096]{2,1,0:T(8,128)(2,1)S(1)}, u32[]{:S(2)}, u32[]{:S(2)}) collective-permute-start(bf16[2,16,4096]{2,1,0:T(8,128)(2,1)} %get-tuple-element.927), channel_id=1, source_target_pairs={{0,2},{2,4},{4,6},{6,8},{8,10},{10,12},{12,14},{14,16},{16,18},{18... | collective-permute-start | bytes 786440 | tf_op jit(solution)/shard_map/while/body/eval_jaxpr/ppermute | solution.py:24
  208.9 10.2 %collective-permute-start = (bf16[2,16,4096]{2,1,0:T(8,128)(2,1)}, bf16[2,16,4096]{2,1,0:T(8,128)(2,1)S(1)}, u32[]{:S(2)}, u32[]{:S(2)}) collective-permute-start(bf16[2,16,4096]{2,1,0:T(8,128)(2,1)} %get-tuple-element.927), channel_id=1, source_target_pairs={{0,2},{2,4},{4,6},{6,8},{8,10},{10,12},{12,14},{14,16},{16,18},{18... | collective-permute-start | bytes 786440 | tf_op jit(solution)/shard_map/while/body/eval_jaxpr/ppermute | solution.py:24
  221.6 8.3 %collective-permute-start = (bf16[2,16,4096]{2,1,0:T(8,128)(2,1)}, bf16[2,16,4096]{2,1,0:T(8,128)(2,1)S(1)}, u32[]{:S(2)}, u32[]{:S(2)}) collective-permute-start(bf16[2,16,4096]{2,1,0:T(8,128)(2,1)} %get-tuple-element.927), channel_id=1, source_target_pairs={{0,2},{2,4},{4,6},{6,8},{8,10},{10,12},{12,14},{14,16},{16,18},{18... | collective-permute-start | bytes 786440 | tf_op jit(solution)/shard_map/while/body/eval_jaxpr/ppermute | solution.py:24
  232.5 8.9 %collective-permute-start = (bf16[2,16,4096]{2,1,0:T(8,128)(2,1)}, bf16[2,16,4096]{2,1,0:T(8,128)(2,1)S(1)}, u32[]{:S(2)}, u32[]{:S(2)}) collective-permute-start(bf16[2,16,4096]{2,1,0:T(8,128)(2,1)} %get-tuple-element.927), channel_id=1, source_target_pairs={{0,2},{2,4},{4,6},{6,8},{8,10},{10,12},{12,14},{14,16},{16,18},{18... | collective-permute-start | bytes 786440 | tf_op jit(solution)/shard_map/while/body/eval_jaxpr/ppermute | solution.py:24
  243.9 8.9 %collective-permute-start = (bf16[2,16,4096]{2,1,0:T(8,128)(2,1)}, bf16[2,16,4096]{2,1,0:T(8,128)(2,1)S(1)}, u32[]{:S(2)}, u32[]{:S(2)}) collective-permute-start(bf16[2,16,4096]{2,1,0:T(8,128)(2,1)} %get-tuple-element.927), channel_id=1, source_target_pairs={{0,2},{2,4},{4,6},{6,8},{8,10},{10,12},{12,14},{14,16},{16,18},{18... | collective-permute-start | bytes 786440 | tf_op jit(solution)/shard_map/while/body/eval_jaxpr/ppermute | solution.py:24
  255.3 8.9 %collective-permute-start = (bf16[2,16,4096]{2,1,0:T(8,128)(2,1)}, bf16[2,16,4096]{2,1,0:T(8,128)(2,1)S(1)}, u32[]{:S(2)}, u32[]{:S(2)}) collective-permute-start(bf16[2,16,4096]{2,1,0:T(8,128)(2,1)} %get-tuple-element.927), channel_id=1, source_target_pairs={{0,2},{2,4},{4,6},{6,8},{8,10},{10,12},{12,14},{14,16},{16,18},{18... | collective-permute-start | bytes 786440 | tf_op jit(solution)/shard_map/while/body/eval_jaxpr/ppermute | solution.py:24
  266.7 9.1 %collective-permute-start.1 = (bf16[2,16,4096]{2,1,0:T(8,128)(2,1)S(1)}, bf16[2,16,4096]{2,1,0:T(8,128)(2,1)}, u32[]{:S(2)}, u32[]{:S(2)}) collective-permute-start(bf16[2,16,4096]{2,1,0:T(8,128)(2,1)S(1)} %get-tuple-element.831), channel_id=1, source_target_pairs={{2,0},{4,2},{6,4},{8,6},{10,8},{12,10},{14,12},{16,14},{18,16},{20... | collective-permute-start | bytes 786440 | tf_op jit(solution)/shard_map/while/body/eval_jaxpr/ppermute | solution.py:24
  275.9 8.8 %collective-permute-start.1 = (bf16[2,16,4096]{2,1,0:T(8,128)(2,1)S(1)}, bf16[2,16,4096]{2,1,0:T(8,128)(2,1)}, u32[]{:S(2)}, u32[]{:S(2)}) collective-permute-start(bf16[2,16,4096]{2,1,0:T(8,128)(2,1)S(1)} %get-tuple-element.831), channel_id=1, source_target_pairs={{2,0},{4,2},{6,4},{8,6},{10,8},{12,10},{14,12},{16,14},{18,16},{20... | collective-permute-start | bytes 786440 | tf_op jit(solution)/shard_map/while/body/eval_jaxpr/ppermute | solution.py:24
  284.7 11.5 %collective-permute-start.1 = (bf16[2,16,4096]{2,1,0:T(8,128)(2,1)S(1)}, bf16[2,16,4096]{2,1,0:T(8,128)(2,1)}, u32[]{:S(2)}, u32[]{:S(2)}) collective-permute-start(bf16[2,16,4096]{2,1,0:T(8,128)(2,1)S(1)} %get-tuple-element.831), channel_id=1, source_target_pairs={{2,0},{4,2},{6,4},{8,6},{10,8},{12,10},{14,12},{16,14},{18,16},{20... | collective-permute-start | bytes 786440 | tf_op jit(solution)/shard_map/while/body/eval_jaxpr/ppermute | solution.py:24
  296.2 10.3 %collective-permute-start.1 = (bf16[2,16,4096]{2,1,0:T(8,128)(2,1)S(1)}, bf16[2,16,4096]{2,1,0:T(8,128)(2,1)}, u32[]{:S(2)}, u32[]{:S(2)}) collective-permute-start(bf16[2,16,4096]{2,1,0:T(8,128)(2,1)S(1)} %get-tuple-element.831), channel_id=1, source_target_pairs={{2,0},{4,2},{6,4},{8,6},{10,8},{12,10},{14,12},{16,14},{18,16},{20... | collective-permute-start | bytes 786440 | tf_op jit(solution)/shard_map/while/body/eval_jaxpr/ppermute | solution.py:24
  306.6 7.9 %collective-permute-start.1 = (bf16[2,16,4096]{2,1,0:T(8,128)(2,1)S(1)}, bf16[2,16,4096]{2,1,0:T(8,128)(2,1)}, u32[]{:S(2)}, u32[]{:S(2)}) collective-permute-start(bf16[2,16,4096]{2,1,0:T(8,128)(2,1)S(1)} %get-tuple-element.831), channel_id=1, source_target_pairs={{2,0},{4,2},{6,4},{8,6},{10,8},{12,10},{14,12},{16,14},{18,16},{20... | collective-permute-start | bytes 786440 | tf_op jit(solution)/shard_map/while/body/eval_jaxpr/ppermute | solution.py:24
  314.5 7.2 %collective-permute-start.1 = (bf16[2,16,4096]{2,1,0:T(8,128)(2,1)S(1)}, bf16[2,16,4096]{2,1,0:T(8,128)(2,1)}, u32[]{:S(2)}, u32[]{:S(2)}) collective-permute-start(bf16[2,16,4096]{2,1,0:T(8,128)(2,1)S(1)} %get-tuple-element.831), channel_id=1, source_target_pairs={{2,0},{4,2},{6,4},{8,6},{10,8},{12,10},{14,12},{16,14},{18,16},{20... | collective-permute-start | bytes 786440 | tf_op jit(solution)/shard_map/while/body/eval_jaxpr/ppermute | solution.py:24
  321.8 7.2 %collective-permute-start.1 = (bf16[2,16,4096]{2,1,0:T(8,128)(2,1)S(1)}, bf16[2,16,4096]{2,1,0:T(8,128)(2,1)}, u32[]{:S(2)}, u32[]{:S(2)}) collective-permute-start(bf16[2,16,4096]{2,1,0:T(8,128)(2,1)S(1)} %get-tuple-element.831), channel_id=1, source_target_pairs={{2,0},{4,2},{6,4},{8,6},{10,8},{12,10},{14,12},{16,14},{18,16},{20... | collective-permute-start | bytes 786440 | tf_op jit(solution)/shard_map/while/body/eval_jaxpr/ppermute | solution.py:24
  329.1 14.3 %collective-permute-start.1 = (bf16[2,16,4096]{2,1,0:T(8,128)(2,1)S(1)}, bf16[2,16,4096]{2,1,0:T(8,128)(2,1)}, u32[]{:S(2)}, u32[]{:S(2)}) collective-permute-start(bf16[2,16,4096]{2,1,0:T(8,128)(2,1)S(1)} %get-tuple-element.831), channel_id=1, source_target_pairs={{2,0},{4,2},{6,4},{8,6},{10,8},{12,10},{14,12},{16,14},{18,16},{20... | collective-permute-start | bytes 786440 | tf_op jit(solution)/shard_map/while/body/eval_jaxpr/ppermute | solution.py:24
  343.4 8.4 %collective-permute-start.1 = (bf16[2,16,4096]{2,1,0:T(8,128)(2,1)S(1)}, bf16[2,16,4096]{2,1,0:T(8,128)(2,1)}, u32[]{:S(2)}, u32[]{:S(2)}) collective-permute-start(bf16[2,16,4096]{2,1,0:T(8,128)(2,1)S(1)} %get-tuple-element.831), channel_id=1, source_target_pairs={{2,0},{4,2},{6,4},{8,6},{10,8},{12,10},{14,12},{16,14},{18,16},{20... | collective-permute-start | bytes 786440 | tf_op jit(solution)/shard_map/while/body/eval_jaxpr/ppermute | solution.py:24
  351.8 8.0 %collective-permute-start.1 = (bf16[2,16,4096]{2,1,0:T(8,128)(2,1)S(1)}, bf16[2,16,4096]{2,1,0:T(8,128)(2,1)}, u32[]{:S(2)}, u32[]{:S(2)}) collective-permute-start(bf16[2,16,4096]{2,1,0:T(8,128)(2,1)S(1)} %get-tuple-element.831), channel_id=1, source_target_pairs={{2,0},{4,2},{6,4},{8,6},{10,8},{12,10},{14,12},{16,14},{18,16},{20... | collective-permute-start | bytes 786440 | tf_op jit(solution)/shard_map/while/body/eval_jaxpr/ppermute | solution.py:24
  359.9 8.4 %collective-permute-start.1 = (bf16[2,16,4096]{2,1,0:T(8,128)(2,1)S(1)}, bf16[2,16,4096]{2,1,0:T(8,128)(2,1)}, u32[]{:S(2)}, u32[]{:S(2)}) collective-permute-start(bf16[2,16,4096]{2,1,0:T(8,128)(2,1)S(1)} %get-tuple-element.831), channel_id=1, source_target_pairs={{2,0},{4,2},{6,4},{8,6},{10,8},{12,10},{14,12},{16,14},{18,16},{20... | collective-permute-start | bytes 786440 | tf_op jit(solution)/shard_map/while/body/eval_jaxpr/ppermute | solution.py:24
  368.3 9.6 %collective-permute-start.1 = (bf16[2,16,4096]{2,1,0:T(8,128)(2,1)S(1)}, bf16[2,16,4096]{2,1,0:T(8,128)(2,1)}, u32[]{:S(2)}, u32[]{:S(2)}) collective-permute-start(bf16[2,16,4096]{2,1,0:T(8,128)(2,1)S(1)} %get-tuple-element.831), channel_id=1, source_target_pairs={{2,0},{4,2},{6,4},{8,6},{10,8},{12,10},{14,12},{16,14},{18,16},{20... | collective-permute-start | bytes 786440 | tf_op jit(solution)/shard_map/while/body/eval_jaxpr/ppermute | solution.py:24
  378.0 11.1 %collective-permute-start.1 = (bf16[2,16,4096]{2,1,0:T(8,128)(2,1)S(1)}, bf16[2,16,4096]{2,1,0:T(8,128)(2,1)}, u32[]{:S(2)}, u32[]{:S(2)}) collective-permute-start(bf16[2,16,4096]{2,1,0:T(8,128)(2,1)S(1)} %get-tuple-element.831), channel_id=1, source_target_pairs={{2,0},{4,2},{6,4},{8,6},{10,8},{12,10},{14,12},{16,14},{18,16},{20... | collective-permute-start | bytes 786440 | tf_op jit(solution)/shard_map/while/body/eval_jaxpr/ppermute | solution.py:24
  389.1 11.9 %collective-permute-start.1 = (bf16[2,16,4096]{2,1,0:T(8,128)(2,1)S(1)}, bf16[2,16,4096]{2,1,0:T(8,128)(2,1)}, u32[]{:S(2)}, u32[]{:S(2)}) collective-permute-start(bf16[2,16,4096]{2,1,0:T(8,128)(2,1)S(1)} %get-tuple-element.831), channel_id=1, source_target_pairs={{2,0},{4,2},{6,4},{8,6},{10,8},{12,10},{14,12},{16,14},{18,16},{20... | collective-permute-start | bytes 786440 | tf_op jit(solution)/shard_map/while/body/eval_jaxpr/ppermute | solution.py:24
  401.1 89.8 %collective-permute-start.1 = (bf16[2,16,4096]{2,1,0:T(8,128)(2,1)S(1)}, bf16[2,16,4096]{2,1,0:T(8,128)(2,1)}, u32[]{:S(2)}, u32[]{:S(2)}) collective-permute-start(bf16[2,16,4096]{2,1,0:T(8,128)(2,1)S(1)} %get-tuple-element.831), channel_id=1, source_target_pairs={{2,0},{4,2},{6,4},{8,6},{10,8},{12,10},{14,12},{16,14},{18,16},{20... | collective-permute-start | bytes 786440 | tf_op jit(solution)/shard_map/while/body/eval_jaxpr/ppermute | solution.py:24
  491.0 5.3 copy-start.1
  497.9 8.4 %collective-permute-start.1 = (bf16[2,16,4096]{2,1,0:T(8,128)(2,1)S(1)}, bf16[2,16,4096]{2,1,0:T(8,128)(2,1)}, u32[]{:S(2)}, u32[]{:S(2)}) collective-permute-start(bf16[2,16,4096]{2,1,0:T(8,128)(2,1)S(1)} %get-tuple-element.831), channel_id=1, source_target_pairs={{2,0},{4,2},{6,4},{8,6},{10,8},{12,10},{14,12},{16,14},{18,16},{20... | collective-permute-start | bytes 786440 | tf_op jit(solution)/shard_map/while/body/eval_jaxpr/ppermute | solution.py:24
  506.5 5.3 copy-start.1
  513.3 9.9 %collective-permute-start.1 = (bf16[2,16,4096]{2,1,0:T(8,128)(2,1)S(1)}, bf16[2,16,4096]{2,1,0:T(8,128)(2,1)}, u32[]{:S(2)}, u32[]{:S(2)}) collective-permute-start(bf16[2,16,4096]{2,1,0:T(8,128)(2,1)S(1)} %get-tuple-element.831), channel_id=1, source_target_pairs={{2,0},{4,2},{6,4},{8,6},{10,8},{12,10},{14,12},{16,14},{18,16},{20... | collective-permute-start | bytes 786440 | tf_op jit(solution)/shard_map/while/body/eval_jaxpr/ppermute | solution.py:24
  523.3 5.3 copy-start.1
  530.2 11.3 %collective-permute-start.1 = (bf16[2,16,4096]{2,1,0:T(8,128)(2,1)S(1)}, bf16[2,16,4096]{2,1,0:T(8,128)(2,1)}, u32[]{:S(2)}, u32[]{:S(2)}) collective-permute-start(bf16[2,16,4096]{2,1,0:T(8,128)(2,1)S(1)} %get-tuple-element.831), channel_id=1, source_target_pairs={{2,0},{4,2},{6,4},{8,6},{10,8},{12,10},{14,12},{16,14},{18,16},{20... | collective-permute-start | bytes 786440 | tf_op jit(solution)/shard_map/while/body/eval_jaxpr/ppermute | solution.py:24
  541.6 5.3 copy-start.1
  548.4 8.2 %collective-permute-start.1 = (bf16[2,16,4096]{2,1,0:T(8,128)(2,1)S(1)}, bf16[2,16,4096]{2,1,0:T(8,128)(2,1)}, u32[]{:S(2)}, u32[]{:S(2)}) collective-permute-start(bf16[2,16,4096]{2,1,0:T(8,128)(2,1)S(1)} %get-tuple-element.831), channel_id=1, source_target_pairs={{2,0},{4,2},{6,4},{8,6},{10,8},{12,10},{14,12},{16,14},{18,16},{20... | collective-permute-start | bytes 786440 | tf_op jit(solution)/shard_map/while/body/eval_jaxpr/ppermute | solution.py:24
  (17 other events, 11.8 us)
where the time goes:
time: 630 us; the launch traced here: 628 us
  waiting for transfers between devices  284 us (45%)
  starting transfers between devices  139 us (22%)
  blocking collectives  68.3 us (11%)
  local copies, waits for them, and re-layouts  49.9 us (8%)
  other arithmetic  47.1 us (7%)
  matrix products  36.2 us (6%)
    ppermute x38, waiting for transfers between devices, passed_along(): return lax.ppermute(array, axis, pairs)  283 us
    ppermute x38, starting transfers between devices, passed_along(): return lax.ppermute(array, axis, pairs)  121 us
    all_to_all x1, blocking collectives, sent_to_all(): return lax.all_to_all(copies, axis, split_axis=0, concat_axis=0, tiled=True)  68.3 us
    dot_general x12, matrix products, attend(): jnp.dot(normed, w_layer, preferred_element_type=jnp.float32)  24.9 us
    dynamic_update_slice x19, other arithmetic, forward_tick(): lax.dynamic_update_index_in_dim(saved, jnp.where(valid, entering, kept),...  20.4 us
    dynamic_slice x19, local copies, waits for them, and re-layouts, backward_tick(): kept = lax.dynamic_index_in_dim(grads_x, clipped, 0, keepdims=False)  18.5 us
    all_to_all x1, starting transfers between devices, in_one_piece(): lax.all_to_all(both, axis, split_axis=split_dim, concat_axis=concat_dim,...  17.8 us
    dynamic_update_slice x19, other arithmetic, backward_tick(): lax.dynamic_update_index_in_dim(grads_x, jnp.where(valid, sending, kept),...  14.7 us
  transfers between devices with their start and end apart: 39, of which 39 were waited for; matrix products, arithmetic and copies ran while one was open for 5% of the time, Pallas kernels for 0%

commit v1 on v0

v1 whole, which is shorter than its diff:
```python
import functools
import math

import jax
import jax.numpy as jnp
from jax import lax
from jax.experimental import pallas as pl
from jax.experimental.pallas import tpu as pltpu
from jax.sharding import PartitionSpec as P

MESH = pl.DeviceIdType.MESH
F32 = jnp.float32
BF16 = jnp.bfloat16
CHUNK = 256
BLOCK = 16
AHEAD = 6


def nn(a, b):
    return lax.dot_general(a, b, (((1,), (0,)), ((), ())), preferred_element_type=F32)


def nt(a, b):
    return lax.dot_general(a, b, (((1,), (1,)), ((), ())), preferred_element_type=F32)


def chain_kernel(
    sections, width, spread,
    zt0_ref, et_ref, n0_ref, bias_ref, bg_ref, wqkv_ref, wout_ref, gain_ref, x0_ref, cot_ref,
    out_ref, gsum_ref,
    bgt, zt, a_in, a_own, n_in, n_out, f_in, f_out, s_in, s_out,
    x_in, x_out, c_in,
    mt, m_tok, a_tok, beta_cols,
    q_s, k_s, v_s, p_s, y_s, r_s,
    a_send, a_recv, n_send, n_recv, f_send, f_recv, s_send, s_recv,
    x_send, x_recv, c_send, c_recv,
):
    me = lax.axis_index("section")
    last = sections - 1
    up = lax.rem(me + 1, sections)
    down = lax.rem(me + sections - 1, sections)
    head = a_own.shape[0]
    chunks, tokens, wide = x_in.shape
    rows_in_head = head // BLOCK
    scale = 1.0 / math.sqrt(head)

    barrier = pltpu.get_barrier_semaphore()
    pl.semaphore_signal(barrier, inc=1, device_id={"section": up}, device_id_type=MESH)
    pl.semaphore_signal(barrier, inc=1, device_id={"section": down}, device_id_type=MESH)

    def copy_to(src, dst, ssem, rsem, where):
        return pltpu.make_async_remote_copy(
            src_ref=src, dst_ref=dst, send_sem=ssem, recv_sem=rsem,
            device_id={"section": where}, device_id_type=MESH,
        )

    def a_relay(t):
        return copy_to(a_in.at[t], a_in.at[t], a_send.at[t], a_recv.at[t], up)

    def a_first():
        return copy_to(a_own, a_in.at[me], a_send.at[me], a_recv.at[me], up)

    def n_copy():
        return copy_to(n_out, n_in, n_send, n_recv, up)

    def f_copy(t):
        return copy_to(f_out.at[t], f_in.at[t], f_send.at[t], f_recv.at[t], down)

    def s_copy():
        return copy_to(s_out, s_in, s_send, s_recv, down)

    def x_copy(k):
        return copy_to(x_out.at[k], x_in.at[k], x_send.at[k], x_recv.at[k], up)

    def c_copy(k):
        return copy_to(out_ref.at[k], c_in.at[k], c_send.at[k], c_recv.at[k], down)

    def block_of(t):
        low, high = lax.rem(t, spread), lax.div(t, spread)
        start = pl.multiple_of(low * rows_in_head, rows_in_head)
        return bg_ref[pl.ds(start, rows_in_head), high].reshape(head, 4 * head)

    zt[...] = zt0_ref[...]

    def turn(t, carry):
        bgt[t] = block_of(t).T
        return carry

    lax.fori_loop(0, me, turn, 0)

    @pl.when(me == 0)
    def _():
        n_in[...] = n0_ref[...]
        for k in range(chunks):
            x_in[k] = x0_ref[:, k * wide : (k + 1) * wide]

    @pl.when(me == last)
    def _():
        for k in range(chunks):
            c_in[k] = cot_ref[:, k * wide : (k + 1) * wide]
        s_in[...] = jnp.zeros_like(s_in)
        f_in[last] = jnp.zeros_like(f_in[last])

    pl.semaphore_wait(barrier, 2)

    def gather(t, carry):
        a_relay(t).wait_recv()

        @pl.when(me < last)
        def _():
            a_relay(t).start()

        zt[...] += nn(bgt[t], a_in[t])
        return carry

    lax.fori_loop(0, me, gather, 0)

    @pl.when(me > 0)
    def _():
        n_copy().wait_recv()

    norm = n_in[0:1, :]
    scale_r = lax.rsqrt(jnp.maximum(norm, 0.0) * (1.0 / width) + 1e-05)
    qt = zt[0:head, :] * scale_r
    kt = zt[head : 2 * head, :] * scale_r
    vt = zt[2 * head : 3 * head, :] * scale_r
    yt = zt[3 * head :, :]
    scores = nn(kt.T.astype(BF16), qt.astype(BF16)) * scale + bias_ref[...]
    top = jnp.max(scores, axis=0, keepdims=True)
    weights = jnp.exp(scores - top)
    weights = weights / jnp.sum(weights, axis=0, keepdims=True)
    mixed = nn(vt.astype(BF16), weights.astype(BF16))
    a_own[...] = mixed.astype(BF16)

    @pl.when(me < last)
    def _():
        a_first().start()

    at = a_own[...]
    self_block = block_of(me)[:, 3 * head :]
    y1 = yt + nn(self_block, at)
    moved = norm + jnp.sum(at.astype(F32) * (yt + y1), axis=0, keepdims=True)
    n_out[...] = jnp.broadcast_to(moved, n_out.shape)

    @pl.when(me < last)
    def _():
        n_copy().start()

    q_s[...] = qt
    k_s[...] = kt
    v_s[...] = vt
    p_s[...] = weights
    y_s[...] = y1
    r_s[...] = jnp.broadcast_to(scale_r, r_s.shape)
    a_tok[...] = at.astype(F32).T.astype(BF16)

    def x_step(k, carry):
        @pl.when(me > 0)
        def _():
            x_copy(k).wait_recv()

        @pl.when(me < last)
        def _():
            lane = pl.multiple_of(k * wide, wide)
            grown = x_in[k].astype(F32) + nn(a_tok[...], wout_ref[:, pl.ds(lane, wide)])
            x_out[k] = grown.astype(BF16)
            x_copy(k).start()

        return carry

    pause = jnp.minimum(chunks, AHEAD * (last - me))
    lax.fori_loop(0, pause, x_step, 0)

    @pl.when(me < last)
    def _():
        f_copy(me).wait_recv()
        s_copy().wait_recv()

    summed = s_in[0:1, :]
    dat = et_ref[...] - summed * y_s[...] + f_in[me].astype(F32)
    datb = dat.astype(BF16)
    pt = p_s[...]
    dvt = nt(datb, pt.astype(BF16))
    dpt = nn(v_s[...].T.astype(BF16), datb)
    dst = pt * (dpt - jnp.sum(pt * dpt, axis=0, keepdims=True)) * scale
    dstb = dst.astype(BF16)
    dqt = nn(k_s[...].astype(BF16), dstb)
    dkt = nt(q_s[...].astype(BF16), dstb)
    r = r_s[0:1, :]
    inner = jnp.sum(q_s[...] * dqt + k_s[...] * dkt + v_s[...] * dvt, axis=0, keepdims=True)
    beta = r * r * (1.0 / width) * inner
    mt[0:head, :] = (r * dqt).astype(BF16)
    mt[head : 2 * head, :] = (r * dkt).astype(BF16)
    mt[2 * head : 3 * head, :] = (r * dvt).astype(BF16)
    mt[3 * head :, :] = (-summed * a_own[...].astype(F32)).astype(BF16)
    s_out[...] = jnp.broadcast_to(summed + beta, s_out.shape)

    def f_step(i, carry):
        t = me - 1 - i

        @pl.when(me < last)
        def _():
            f_copy(t).wait_recv()

        @pl.when(me == last)
        def _():
            f_in[t] = jnp.zeros_like(f_in[t])

        f_out[t] = (f_in[t].astype(F32) + nn(block_of(t), mt[...])).astype(BF16)
        f_copy(t).start()

        @pl.when(i == 0)
        def _():
            s_copy().start()

        return carry

    lax.fori_loop(0, me, f_step, 0)

    lax.fori_loop(pause, chunks, x_step, 0)

    m_tok[:, 0:head] = mt[0:head, :].astype(F32).T.astype(BF16)
    m_tok[:, head : 2 * head] = mt[head : 2 * head, :].astype(F32).T.astype(BF16)
    m_tok[:, 2 * head :] = mt[2 * head : 3 * head, :].astype(F32).T.astype(BF16)
    beta_cols[...] = jnp.broadcast_to(beta, (tokens, tokens)).T

    def c_step(k, carry):
        @pl.when(me < last)
        def _():
            c_copy(k).wait_recv()

        start = pl.multiple_of(k * wide, wide)
        turned = nt(m_tok[...], wqkv_ref[pl.ds(start, wide), :])
        x = x_in[k].astype(F32)
        fall = jnp.concatenate([beta_cols[...]] * (wide // tokens), axis=1)
        grad = c_in[k].astype(F32) + gain_ref[k] * turned - fall * x
        gsum_ref[k] = jnp.sum(x * turned, axis=0, keepdims=True)
        out_ref[k] = grad.astype(BF16)

        @pl.when(me > 0)
        def _():
            c_copy(k).start()

        return carry

    lax.fori_loop(0, chunks, c_step, 0)

    @pl.when(me < last)
    def _():
        def done_a(t, carry):
            a_relay(t).wait_send()
            return carry

        lax.fori_loop(0, me + 1, done_a, 0)
        n_copy().wait_send()

        def done_x(k, carry):
            x_copy(k).wait_send()
            return carry

        lax.fori_loop(0, chunks, done_x, 0)

    @pl.when(me > 0)
    def _():
        def done_f(t, carry):
            f_copy(t).wait_send()
            return carry

        lax.fori_loop(0, me, done_f, 0)
        s_copy().wait_send()

        def done_c(k, carry):
            c_copy(k).wait_send()
            return carry

        lax.fori_loop(0, chunks, done_c, 0)


def run_chain(sections, zt0, et, n0, bias, bg, wqkv, wout, gain, x0, cot):
    tokens, width = x0.shape
    head = wout.shape[0]
    chunks = width // CHUNK
    spread = bg.shape[0] * BLOCK // head
    vmem = pl.BlockSpec(memory_space=pltpu.VMEM)
    dma = pltpu.SemaphoreType.DMA
    square = (head, tokens)
    return pl.pallas_call(
        functools.partial(chain_kernel, sections, width, spread),
        out_shape=(
            jax.ShapeDtypeStruct((chunks, tokens, CHUNK), BF16),
            jax.ShapeDtypeStruct((chunks, 1, CHUNK), F32),
        ),
        in_specs=[vmem] * 10,
        out_specs=(vmem, vmem),
        scratch_shapes=[
            pltpu.VMEM((sections, 4 * head, head), BF16),
            pltpu.VMEM((4 * head, tokens), F32),
            pltpu.VMEM((sections, *square), BF16),
            pltpu.VMEM(square, BF16),
            pltpu.VMEM((8, tokens), F32),
            pltpu.VMEM((8, tokens), F32),
            pltpu.VMEM((sections, *square), BF16),
            pltpu.VMEM((sections, *square), BF16),
            pltpu.VMEM((8, tokens), F32),
            pltpu.VMEM((8, tokens), F32),
            pltpu.VMEM((chunks, tokens, CHUNK), BF16),
            pltpu.VMEM((chunks, tokens, CHUNK), BF16),
            pltpu.VMEM((chunks, tokens, CHUNK), BF16),
            pltpu.VMEM((4 * head, tokens), BF16),
            pltpu.VMEM((tokens, 3 * head), BF16),
            pltpu.VMEM((tokens, head), BF16),
            pltpu.VMEM((tokens, tokens), F32),
            pltpu.VMEM(square, F32),
            pltpu.VMEM(square, F32),
            pltpu.VMEM(square, F32),
            pltpu.VMEM((tokens, tokens), F32),
            pltpu.VMEM(square, F32),
            pltpu.VMEM((8, tokens), F32),
            dma((sections,)), dma((sections,)), dma, dma,
            dma((sections,)), dma((sections,)), dma, dma,
            dma((chunks,)), dma((chunks,)), dma((chunks,)), dma((chunks,)),
        ],
        compiler_params=pltpu.CompilerParams(
            collective_id=0, has_side_effects=True, vmem_limit_bytes=48 << 20
        ),
    )(zt0, et, n0, bias, bg, wqkv, wout, gain, x0, cot)


def exchanged(array):
    return lax.all_to_all(array, "group", split_axis=0, concat_axis=0, tiled=True)


def local(tokens_in, cotangent, gains, w_qkv, w_out, segments, plan):
    sections = lax.axis_size("section")
    plane = lax.axis_size(("dp", "group"))
    place = lax.axis_index(("dp", "group"))
    rows_dev = plan.shape[1]
    width = tokens_in.shape[1]
    row_len = segments.shape[1]
    tokens = rows_dev * row_len
    gain, wqkv, wout = gains[0], w_qkv[0], w_out[0]
    head = wout.shape[0]
    chunks = width // CHUNK

    blocks = head // BLOCK
    spread = plane // blocks
    each = sections // spread
    own_rows = lax.dynamic_slice_in_dim(wout, lax.rem(place, blocks) * BLOCK, BLOCK, 0)
    all_rows = lax.all_gather(own_rows, "section").reshape(each, spread, BLOCK, width)
    mine = lax.dynamic_index_in_dim(all_rows, lax.div(place, blocks), 1, keepdims=False)
    scaled = (wqkv.astype(F32) * gain[:, None]).astype(BF16)
    both = jnp.concatenate([scaled, wout.T], axis=1)
    piece = nn(mine.reshape(each * BLOCK, width), both).astype(BF16).reshape(each, BLOCK, 4 * head)
    bg = lax.all_gather(piece, ("dp", "group"))

    rows = jnp.take(tokens_in.reshape(rows_dev, row_len, width), plan[0], axis=0)
    segs = jnp.take(segments, plan[0], axis=0).astype(BF16)
    x0 = exchanged(rows).reshape(tokens, width)
    seg = exchanged(segs).reshape(tokens)

    zt0 = lax.dot_general(both, x0, (((0,), (1,)), ((), ())), preferred_element_type=F32)
    et = nt(wout, cotangent)
    n0 = jnp.broadcast_to(jnp.sum(jnp.square(x0.astype(F32)), axis=1)[None], (8, tokens))
    at = jnp.arange(tokens)
    allowed = (
        (at[:, None] <= at[None, :])
        & (at[:, None] // row_len == at[None, :] // row_len)
        & (seg[:, None] == seg[None, :])
    )
    bias = jnp.where(allowed, 0.0, -1e30).astype(F32)

    grads, gsum = run_chain(
        sections, zt0, et, n0, bias, bg, wqkv, wout, gain.reshape(chunks, 1, CHUNK), x0, cotangent
    )
    grads = grads.transpose(1, 0, 2).reshape(1, tokens, width)
    gain_whole = lax.psum(gsum.reshape(1, width), ("dp", "group"))
    return grads, gain_whole


def solution(mesh):
    placed = (
        P(("dp", "group"), None),
        P(("dp", "group"), None),
        P("section", None),
        P("section", None, None),
        P("section", None, None),
        P(("dp", "group"), None),
        P(("dp", "group"), None),
    )
    return jax.shard_map(
        local,
        mesh=mesh,
        in_specs=placed,
        out_specs=(P("section", ("dp", "group"), None), P("section", None)),
        check_vma=False,
    )
```

time: 630 us -> 608 us (0.965)
  blocking collectives: 68.3 us -> 255 us
  Pallas kernels: 0 us -> 146 us
  waiting for transfers between devices: 284 us -> 145 us
  starting transfers between devices: 139 us -> 17 us
  other arithmetic: 47.1 us -> 6.64 us
  local copies, waits for them, and re-layouts: 49.9 us -> 13.1 us
  matrix products: 36.2 us -> 8.51 us
  between operations: 0.7 us -> 14.2 us
    ppermute x38 -> x0, waiting for transfers between devices: 283 us -> none  [passed_along(): return lax.ppermute(array, axis, pairs)]
    psum x0 -> x1, blocking collectives: none -> 255 us  [local(): gain_whole = lax.psum(gsum.reshape(1, width), ('dp', 'group'))]
    pallas_call x0 -> x1, Pallas kernels: none -> 146 us  [run_chain(): pl.pallas_call(functools.partial(chain_kernel, sections, width, spread),...]
    all_gather x0 -> x2, waiting for transfers between devices: none -> 145 us  [the longest x1 72.8 us: local(): lax.all_gather(own_rows, 'section').reshape(each, spread, BLOCK, width)]
    ppermute x38 -> x0, starting transfers between devices: 121 us -> none  [passed_along(): return lax.ppermute(array, axis, pairs)]
    all_to_all x1 -> x0, blocking collectives: 68.3 us -> none  [sent_to_all(): return lax.all_to_all(copies, axis, split_axis=0, concat_axis=0, tiled=True)]
    dynamic_update_slice x38 -> x0, other arithmetic: 35.1 us -> none  [the longest x19 20.4 us: forward_tick(): lax.dynamic_update_index_in_dim(saved, jnp.where(valid, entering, kept),...]
    dot_general x48 -> x3, matrix products: 36.2 us -> 8.51 us  [the longest x1 3.51 us: local(): lax.dot_general(both, x0, (((0,), (1,)), ((), ())), preferred_element_typ...]
  transfers between devices with their start and end apart: 39 -> 4, of which waited for: 39 -> 3; matrix products, arithmetic and copies ran while one was open for 5% -> 3% of each run, Pallas kernels for 0% -> 0%
where the time goes in v1:
time: 608 us; the launch traced here: 606 us
  blocking collectives  255 us (42%)
  Pallas kernels  146 us (24%)
  waiting for transfers between devices  145 us (24%)
  starting transfers between devices  17 us (3%)
  between operations  14.2 us (2%)
  local copies, waits for them, and re-layouts  13.1 us (2%)
  matrix products  8.51 us (1%)
  other arithmetic  6.64 us (1%)
    psum x1, blocking collectives, local(): gain_whole = lax.psum(gsum.reshape(1, width), ('dp', 'group'))  255 us
    pallas_call x1, Pallas kernels, run_chain(): pl.pallas_call(functools.partial(chain_kernel, sections, width, spread),...  146 us
    all_gather x1, waiting for transfers between devices, local(): lax.all_gather(own_rows, 'section').reshape(each, spread, BLOCK, width)  72.8 us
    all_gather x1, waiting for transfers between devices, local(): bg = lax.all_gather(piece, ('dp', 'group'))  72.1 us
    all_to_all x2, starting transfers between devices, exchanged(): lax.all_to_all(array, 'group', split_axis=0, concat_axis=0, tiled=True)  16.9 us
  transfers between devices with their start and end apart: 4, of which 3 were waited for; matrix products, arithmetic and copies ran while one was open for 3% of the time, Pallas kernels for 0%

profile of v1, /device:TPU:1, one launch (start us, length us, event | category | flops | bytes accessed | tf_op | source)
XLA Modules:
  0.0 605.8 jit_solution(5008647209255791585)
XLA Ops:
  7.2 0.0 copy-start
  7.2 0.0 all-gather.3.cloned.1.call-start
  7.2 1.6 constant_dynamic-slice_fusion.1
  8.9 0.0 all-gather.3.cloned.1.call-update
  8.9 0.0 all-gather.5.cloned.1.call-start
  9.0 1.6 copy.13
  10.6 0.0 copy-start.7
  10.6 3.8 multiply_convert_fusion
  14.4 72.8 %all-gather.3.cloned.1.call-done = bf16[16,16,4096]{2,1,0:T(8,128)(2,1)} async-done(((bf16[1,16,4096]{2,1,0:T(8,128)(2,1)}), bf16[16,16,4096]{2,1,0:T(8,128)(2,1)}) %all-gather.3.cloned.1.call-update) | async-done | bytes 2097168 | tf_op jit(solution)/shard_map/all_gather | solution.py:349
  87.2 1.0 constant_dynamic-slice_fusion
  88.1 0.0 copy-done.7
  88.1 0.0 copy-start.9
  88.1 3.3 fusion.2
  91.5 0.0 all-gather.5.cloned.1.call-update
  91.5 0.0 copy-done.9
  91.5 0.0 copy-done
  91.6 0.0 copy-start.8
  91.6 0.6 gather_fusion
  92.2 0.0 copy-start.1
  92.2 1.1 broadcast_select_fusion
  93.4 13.7 %all-to-all-start = ((bf16[8,16,4096]{2,1,0:T(8,128)(2,1)}), bf16[8,16,4096]{2,1,0:T(8,128)(2,1)S(1)}, u32[]{:S(2)}, u32[]{:S(2)}) async-start(bf16[8,16,4096]{2,1,0:T(8,128)(2,1)} %broadcast_select_fusion), calls=%async_computation | async-start | bytes 2097152 | tf_op jit(solution)/shard_map/all_to_all | solution.py:330
  107.0 0.5 broadcast.129
  107.5 0.7 reduce.4
  108.2 0.1 squeeze.20
  108.3 0.0 copy-done.8
  108.3 0.6 gather_fusion.1
  108.8 0.7 select_convert_fusion
  109.5 0.0 all-to-all-done
  109.5 3.2 all-to-all-start.1
  112.7 0.3 multiply_reduce_fusion
  113.0 0.6 broadcast_in_dim.42
  113.6 0.1 all-to-all-done.1
  113.8 0.1 eq.31
  113.9 0.1 fusion.5.bias_ref
  114.0 1.7 fusion.9.et_ref
  115.6 0.0 copy-start.4
  115.7 3.5 fusion.1.zt0_ref
  119.2 72.1 %all-gather.5.cloned.1.call-done.bg_ref = bf16[64,2,16,512]{3,2,1,0:T(8,128)(2,1)} async-done(((bf16[1,2,16,512]{3,2,1,0:T(8,128)(2,1)}), bf16[64,2,16,512]{3,2,1,0:T(8,128)(2,1)}) %all-gather.5.cloned.1.call-update) | async-done | bytes 2097168 | tf_op jit(solution)/shard_map/all_gather | solution.py:354
  191.3 0.7 broadcast_in_dim.43.n0_ref
  191.9 0.0 copy-done.4
  191.9 1.2 copy-done.2
  193.2 145.9 %shard_map.86 = (bf16[16,128,256]{2,1,0:T(8,128)(2,1)S(1)}, f32[16,1,256]{2,1,0:T(1,128)S(1)}) custom-call(f32[512,128]{1,0:T(8,128)S(1)} %fusion.1.zt0_ref, f32[128,128]{1,0:T(8,128)S(1)} %fusion.9.et_ref, f32[8,128]{1,0:T(8,128)S(1)} %broadcast_in_dim.43.n0_ref, f32[128,128]{1,0:T(8,128)S(1)} %fusion.5.bias_ref, ...), custom_call_target="tpu_custom_call" | custom-call | tf_op jit(solution)/shard_map/pallas_call | solution.py:287
  339.1 0.0 copy-start.3
  339.1 1.0 copy-done.3
  340.0 0.6 copy-done.5
  340.6 1.6 copy.14
  342.3 1.3 copy.15
  343.6 255.4 %psum.7 = f32[1,4096]{1,0:T(1,128)} all-reduce(f32[1,4096]{1,0:T(1,128)S(1)} %bitcast.35), channel_id=1, replica_groups=mesh['dp'=32,'section'=16,'group'=2] {'dp','group'}, use_global_device_ids=true, to_apply=%region_1.2 | all-reduce | flops 4096 | bytes 32768 | tf_op jit(solution)/shard_map/psum | solution.py:376
  (10 shorter events, 0.0 us)
Async XLA Ops:
  7.2 84.4 %copy-start = (bf16[128,4096]{1,0:T(8,128)(2,1)S(1)}, bf16[128,4096]{1,0:T(8,128)(2,1)}, u32[]{:S(2)}) copy-start(bf16[128,4096]{1,0:T(8,128)(2,1)} %param.7) | copy-start | bytes 3145732
  7.2 80.0 %all-gather.3.cloned.1.call-start = ((), (), s32[]{:S(2)}) async-start(), calls=%async_computation.2 | async-start | bytes 2228224 | tf_op jit(solution)/shard_map/all_gather | solution.py:349
  8.9 182.4 %all-gather.5.cloned.1.call-start = ((), (), s32[]{:S(2)}) async-start(), calls=%async_computation.3 | async-start | bytes 2129920 | tf_op jit(solution)/shard_map/all_gather | solution.py:354
  10.6 77.5 %copy-start.7 = (bf16[4096,128]{1,0:T(8,128)(2,1)}, bf16[4096,128]{1,0:T(8,128)(2,1)S(1)}, u32[]{:S(2)}) copy-start(bf16[4096,128]{1,0:T(8,128)(2,1)S(1)} %copy.13) | copy-start | bytes 3145732
  88.1 3.4 copy-start.9
  91.6 16.7 %copy-start.8 = (s32[8,16]{1,0:T(8,128)S(1)}, s32[8,16]{1,0:T(8,128)}, u32[]{:S(2)}) copy-start(s32[8,16]{1,0:T(8,128)} %param.12) | copy-start | bytes 1540
  92.2 21.8 %copy-start.1 = (bf16[1,128,4096]{2,1,0:T(8,128)(2,1)S(1)}, bf16[1,128,4096]{2,1,0:T(8,128)(2,1)}, u32[]{:S(2)}) copy-start(bf16[1,128,4096]{2,1,0:T(8,128)(2,1)} %param.11) | copy-start | bytes 3145732
  93.4 16.2 %all-to-all-start = ((bf16[8,16,4096]{2,1,0:T(8,128)(2,1)}), bf16[8,16,4096]{2,1,0:T(8,128)(2,1)S(1)}, u32[]{:S(2)}, u32[]{:S(2)}) async-start(bf16[8,16,4096]{2,1,0:T(8,128)(2,1)} %broadcast_select_fusion), calls=%async_computation | async-start | bytes 2097152 | tf_op jit(solution)/shard_map/all_to_all | solution.py:330
  109.5 4.3 all-to-all-start.1
  115.6 76.3 %copy-start.4 = (f32[1,4096]{1,0:T(1,128)S(1)}, f32[1,4096]{1,0:T(1,128)}, u32[]{:S(2)}) copy-start(f32[1,4096]{1,0:T(1,128)} %param.9) | copy-start | bytes 49156
  191.9 1.2 copy-start.2
  339.1 1.0 copy-start.3
  340.0 0.6 copy-start.5
  340.6 3.0 copy-start.6
Sparse Core Ops, SparseCore 0:
  11.2 75.8 all-gather.2
  91.7 99.5 all-gather.4

commit v2 on v1

--- a/solution.py
+++ b/solution.py
@@ -13,6 +13,8 @@
 BF16 = jnp.bfloat16
 CHUNK = 256
 BLOCK = 16
+PIECES = 4
+ALONG_X = 4
 AHEAD = 6
 
 
@@ -25,74 +27,154 @@
 
 
 def chain_kernel(
-    sections, width, spread,
-    zt0_ref, et_ref, n0_ref, bias_ref, bg_ref, wqkv_ref, wout_ref, gain_ref, x0_ref, cot_ref,
-    out_ref, gsum_ref,
-    bgt, zt, a_in, a_own, n_in, n_out, f_in, f_out, s_in, s_out,
+    sections, along_y, row_len,
+    rows_ref, segs_ref, wqkv_ref, wout_ref, gain_ref, cot_ref,
+    out_ref, gtotal_ref,
+    x0, seg_in, zb, bg, bgt, zt, et, bias, a_in, a_own, n_in, n_out, f_in, f_out, s_in, s_out,
     x_in, x_out, c_in,
     mt, m_tok, a_tok, beta_cols,
     q_s, k_s, v_s, p_s, y_s, r_s,
+    g_own, g_pair, g_x, g_y,
+    e_send, e_recv, z_send, z_recv, by_send, by_recv, bx_send, bx_recv, bc_send, bc_recv,
     a_send, a_recv, n_send, n_recv, f_send, f_recv, s_send, s_recv,
     x_send, x_recv, c_send, c_recv,
+    gp_send, gp_recv, gx_send, gx_recv, gy_send, gy_recv,
 ):
     me = lax.axis_index("section")
+    place = lax.axis_index("dp")
+    core = lax.axis_index("group")
+    my_y, my_x = lax.div(place, ALONG_X), lax.rem(place, ALONG_X)
     last = sections - 1
     up = lax.rem(me + 1, sections)
     down = lax.rem(me + sections - 1, sections)
+    other = 1 - core
     head = a_own.shape[0]
     chunks, tokens, wide = x_in.shape
-    rows_in_head = head // BLOCK
+    width = chunks * wide
+    each = sections // along_y
+    mine = core * ALONG_X + my_x
     scale = 1.0 / math.sqrt(head)
 
+    def y_peer(d):
+        return lax.rem(my_y + d, along_y) * ALONG_X + my_x
+
+    def x_peer(d):
+        return my_y * ALONG_X + lax.rem(my_x + d, ALONG_X)
+
     barrier = pltpu.get_barrier_semaphore()
-    pl.semaphore_signal(barrier, inc=1, device_id={"section": up}, device_id_type=MESH)
-    pl.semaphore_signal(barrier, inc=1, device_id={"section": down}, device_id_type=MESH)
+    peers = [{"section": up}, {"section": down}, {"group": other}]
+    peers += [{"dp": y_peer(d)} for d in range(1, along_y)]
+    peers += [{"dp": x_peer(d)} for d in range(1, ALONG_X)]
+    for peer in peers:
+        pl.semaphore_signal(barrier, inc=1, device_id=peer, device_id_type=MESH)
 
     def copy_to(src, dst, ssem, rsem, where):
         return pltpu.make_async_remote_copy(
             src_ref=src, dst_ref=dst, send_sem=ssem, recv_sem=rsem,
-            device_id={"section": where}, device_id_type=MESH,
+            device_id=where, device_id_type=MESH,
+        )
+
+    def rows_copy():
+        return copy_to(
+            rows_ref.at[other], x0.at[core], e_send.at[0], e_recv.at[0], {"group": other}
+        )
+
+    def segs_copy():
+        return copy_to(
+            segs_ref.at[other], seg_in.at[core], e_send.at[1], e_recv.at[1], {"group": other}
+        )
+
+    def z_copy(h, p):
+        return copy_to(
+            zb.at[h, p], zb.at[h, p], z_send.at[h, p], z_recv.at[h, p], {"section": up}
+        )
+
+    def by_copy(h, d):
+        t = my_y + along_y * h
+        return copy_to(
+            bg.at[t, mine], bg.at[t, mine], by_send.at[h, d], by_recv.at[t], {"dp": y_peer(d)}
+        )
+
+    def by_arrival(t):
+        return copy_to(
+            bg.at[t, mine], bg.at[t, mine], by_send.at[0, 0], by_recv.at[t], {"dp": y_peer(1)}
+        )
+
+    def bx_copy(t, d):
+        return copy_to(
+            bg.at[t, mine], bg.at[t, mine], bx_send.at[t, d], bx_recv.at[t, d], {"dp": x_peer(d)}
+        )
+
+    def bc_copy(t):
+        half = pl.ds(core * ALONG_X, ALONG_X)
+        return copy_to(
+            bg.at[t, half], bg.at[t, half], bc_send.at[t], bc_recv.at[t], {"group": other}
         )
 
     def a_relay(t):
-        return copy_to(a_in.at[t], a_in.at[t], a_send.at[t], a_recv.at[t], up)
+        return copy_to(a_in.at[t], a_in.at[t], a_send.at[t], a_recv.at[t], {"section": up})
 
     def a_first():
-        return copy_to(a_own, a_in.at[me], a_send.at[me], a_recv.at[me], up)
+        return copy_to(a_own, a_in.at[me], a_send.at[me], a_recv.at[me], {"section": up})
 
     def n_copy():
-        return copy_to(n_out, n_in, n_send, n_recv, up)
+        return copy_to(n_out, n_in, n_send, n_recv, {"section": up})
 
     def f_copy(t):
-        return copy_to(f_out.at[t], f_in.at[t], f_send.at[t], f_recv.at[t], down)
+        return copy_to(f_out.at[t], f_in.at[t], f_send.at[t], f_recv.at[t], {"section": down})
 
     def s_copy():
-        return copy_to(s_out, s_in, s_send, s_recv, down)
+        return copy_to(s_out, s_in, s_send, s_recv, {"section": down})
 
     def x_copy(k):
-        return copy_to(x_out.at[k], x_in.at[k], x_send.at[k], x_recv.at[k], up)
+        return copy_to(x_out.at[k], x_in.at[k], x_send.at[k], x_recv.at[k], {"section": up})
+
+    def lanes(k):
+        return pl.ds(pl.multiple_of(k * wide, wide), wide)
 
     def c_copy(k):
-        return copy_to(out_ref.at[k], c_in.at[k], c_send.at[k], c_recv.at[k], down)
+        return copy_to(
+            out_ref.at[:, lanes(k)], c_in.at[k], c_send.at[k], c_recv.at[k], {"section": down}
+        )
+
+    def gp_copy():
+        return copy_to(g_own, g_pair, gp_send, gp_recv, {"group": other})
+
+    def gx_copy(d):
+        return copy_to(
+            g_x.at[my_x], g_x.at[my_x], gx_send.at[d], gx_recv.at[d], {"dp": x_peer(d)}
+        )
+
+    def gy_copy(d):
+        return copy_to(
+            g_y.at[my_y], g_y.at[my_y], gy_send.at[d], gy_recv.at[d], {"dp": y_peer(d)}
+        )
 
     def block_of(t):
-        low, high = lax.rem(t, spread), lax.div(t, spread)
-        start = pl.multiple_of(low * rows_in_head, rows_in_head)
-        return bg_ref[pl.ds(start, rows_in_head), high].reshape(head, 4 * head)
-
-    zt[...] = zt0_ref[...]
-
-    def turn(t, carry):
-        bgt[t] = block_of(t).T
-        return carry
-
-    lax.fori_loop(0, me, turn, 0)
-
-    @pl.when(me == 0)
-    def _():
-        n_in[...] = n0_ref[...]
-        for k in range(chunks):
-            x_in[k] = x0_ref[:, k * wide : (k + 1) * wide]
+        return bg[t].reshape(head, 4 * head)
+
+    piece = width // PIECES
+    for h in range(each):
+
+        @pl.when(me == my_y + along_y * h)
+        def _():
+            start = pl.multiple_of(mine * BLOCK, BLOCK)
+            for p in range(PIECES):
+                zb[h, p] = wout_ref[pl.ds(start, BLOCK), p * piece : (p + 1) * piece]
+
+    pl.semaphore_wait(barrier, len(peers))
+    rows_copy().start()
+    segs_copy().start()
+    for h in range(each):
+
+        @pl.when((me == my_y + along_y * h) & (me < last))
+        def _():
+            for p in range(PIECES):
+                z_copy(h, p).start()
+
+    x0[core] = rows_ref[core]
+    seg_in[core] = segs_ref[core]
+    et[...] = nt(wout_ref[...], cot_ref[...])
 
     @pl.when(me == last)
     def _():
@@ -101,7 +183,88 @@
         s_in[...] = jnp.zeros_like(s_in)
         f_in[last] = jnp.zeros_like(f_in[last])
 
-    pl.semaphore_wait(barrier, 2)
+    rows_copy().wait_recv()
+    segs_copy().wait_recv()
+
+    segment = seg_in[0][0:8, :].astype(F32) + seg_in[1][0:8, :].astype(F32)
+    of_query = jnp.broadcast_to(segment[0:1, :], (tokens, tokens))
+    of_key = of_query.T
+    key = lax.broadcasted_iota(jnp.int32, (tokens, tokens), 0)
+    query = lax.broadcasted_iota(jnp.int32, (tokens, tokens), 1)
+    allowed = (key <= query) & (key // row_len == query // row_len) & (of_key == of_query)
+    bias[...] = jnp.where(allowed, 0.0, -1e30)
+
+    square = jnp.zeros((tokens, 128), F32)
+    grown = jnp.zeros((tokens, 3 * head), F32)
+    outer = jnp.zeros((head, tokens), F32)
+    for p in range(PIECES):
+        cut = slice(p * piece, (p + 1) * piece)
+        x = x0[:, :, cut].reshape(tokens, piece)
+        wide_x = x.astype(F32)
+        grown += nn((wide_x * gain_ref[0:1, cut]).astype(BF16), wqkv_ref[cut, :])
+        outer += nt(wout_ref[:, cut], x)
+        for i in range(piece // 128):
+            part = wide_x[:, i * 128 : (i + 1) * 128]
+            square += part * part
+    zt[0 : 3 * head, :] = grown.T
+    zt[3 * head :, :] = outer
+
+    @pl.when(me == 0)
+    def _():
+        n_in[...] = jnp.sum(square.T, axis=0, keepdims=True) + jnp.zeros_like(n_in)
+        for k in range(chunks):
+            x_in[k] = x0[:, :, k * wide : (k + 1) * wide].reshape(tokens, wide)
+
+    for h in reversed(range(each)):
+        source = my_y + along_y * h
+
+        @pl.when(me > source)
+        def _():
+            for p in range(PIECES):
+                z_copy(h, p).wait_recv()
+
+                @pl.when(me < last)
+                def _():
+                    z_copy(h, p).start()
+
+        @pl.when(me >= source)
+        def _():
+            left = jnp.zeros((BLOCK, 3 * head), F32)
+            right = jnp.zeros((BLOCK, head), F32)
+            for p in range(PIECES):
+                cut = slice(p * piece, (p + 1) * piece)
+                rows = zb[h, p]
+                left += nn((rows.astype(F32) * gain_ref[0:1, cut]).astype(BF16), wqkv_ref[cut, :])
+                right += nt(rows, wout_ref[:, cut])
+            bg[source, mine] = jnp.concatenate([left, right], axis=1).astype(BF16)
+            for d in range(1, along_y):
+                by_copy(h, d).start()
+
+    def over_x(t, carry):
+        @pl.when(lax.rem(t, along_y) != my_y)
+        def _():
+            by_arrival(t).wait_recv()
+
+        for d in range(1, ALONG_X):
+            bx_copy(t, d).start()
+        return carry
+
+    lax.fori_loop(0, me + 1, over_x, 0)
+
+    def over_cores(t, carry):
+        for d in range(1, ALONG_X):
+            bx_copy(t, d).wait_recv()
+        bc_copy(t).start()
+        return carry
+
+    lax.fori_loop(0, me + 1, over_cores, 0)
+
+    def turn(t, carry):
+        bc_copy(t).wait_recv()
+        bgt[t] = block_of(t).T
+        return carry
+
+    lax.fori_loop(0, me + 1, turn, 0)
 
     def gather(t, carry):
         a_relay(t).wait_recv()
@@ -125,7 +288,7 @@
     kt = zt[head : 2 * head, :] * scale_r
     vt = zt[2 * head : 3 * head, :] * scale_r
     yt = zt[3 * head :, :]
-    scores = nn(kt.T.astype(BF16), qt.astype(BF16)) * scale + bias_ref[...]
+    scores = nn(kt.T.astype(BF16), qt.astype(BF16)) * scale + bias[...]
     top = jnp.max(scores, axis=0, keepdims=True)
     weights = jnp.exp(scores - top)
     weights = weights / jnp.sum(weights, axis=0, keepdims=True)
@@ -161,9 +324,8 @@
 
         @pl.when(me < last)
         def _():
-            lane = pl.multiple_of(k * wide, wide)
-            grown = x_in[k].astype(F32) + nn(a_tok[...], wout_ref[:, pl.ds(lane, wide)])
-            x_out[k] = grown.astype(BF16)
+            longer = x_in[k].astype(F32) + nn(a_tok[...], wout_ref[:, lanes(k)])
+            x_out[k] = longer.astype(BF16)
             x_copy(k).start()
 
         return carry
@@ -177,7 +339,7 @@
         s_copy().wait_recv()
 
     summed = s_in[0:1, :]
-    dat = et_ref[...] - summed * y_s[...] + f_in[me].astype(F32)
+    dat = et[...] - summed * y_s[...] + f_in[me].astype(F32)
     datb = dat.astype(BF16)
     pt = p_s[...]
     dvt = nt(datb, pt.astype(BF16))
@@ -233,9 +395,9 @@
         turned = nt(m_tok[...], wqkv_ref[pl.ds(start, wide), :])
         x = x_in[k].astype(F32)
         fall = jnp.concatenate([beta_cols[...]] * (wide // tokens), axis=1)
-        grad = c_in[k].astype(F32) + gain_ref[k] * turned - fall * x
-        gsum_ref[k] = jnp.sum(x * turned, axis=0, keepdims=True)
-        out_ref[k] = grad.astype(BF16)
+        grad = c_in[k].astype(F32) + gain_ref[0:1, lanes(k)] * turned - fall * x
+        g_own[pl.ds(k, 1), :] = jnp.sum(x * turned, axis=0, keepdims=True)
+        out_ref[:, lanes(k)] = grad.astype(BF16)
 
         @pl.when(me > 0)
         def _():
@@ -244,6 +406,53 @@
         return carry
 
     lax.fori_loop(0, chunks, c_step, 0)
+
+    gp_copy().start()
+    gp_copy().wait_recv()
+    g_x[my_x] = g_own[...] + g_pair[...]
+    for d in range(1, ALONG_X):
+        gx_copy(d).start()
+    for d in range(1, ALONG_X):
+        gx_copy(d).wait_recv()
+    total = g_x[0]
+    for i in range(1, ALONG_X):
+        total += g_x[i]
+    g_y[my_y] = total
+    for d in range(1, along_y):
+        gy_copy(d).start()
+    for d in range(1, along_y):
+        gy_copy(d).wait_recv()
+    total = g_y[0]
+    for i in range(1, along_y):
+        total += g_y[i]
+    gtotal_ref[...] = total
+
+    rows_copy().wait_send()
+    segs_copy().wait_send()
+    gp_copy().wait_send()
+    for d in range(1, ALONG_X):
+        gx_copy(d).wait_send()
+    for d in range(1, along_y):
+        gy_copy(d).wait_send()
+    for h in range(each):
+
+        @pl.when(me >= my_y + along_y * h)
+        def _():
+            for d in range(1, along_y):
+                by_copy(h, d).wait_send()
+
+            @pl.when(me < last)
+            def _():
+                for p in range(PIECES):
+                    z_copy(h, p).wait_send()
+
+    def done_b(t, carry):
+        for d in range(1, ALONG_X):
+            bx_copy(t, d).wait_send()
+        bc_copy(t).wait_send()
+        return carry
+
+    lax.fori_loop(0, me + 1, done_b, 0)
 
     @pl.when(me < last)
     def _():
@@ -276,25 +485,32 @@
         lax.fori_loop(0, chunks, done_c, 0)
 
 
-def run_chain(sections, zt0, et, n0, bias, bg, wqkv, wout, gain, x0, cot):
-    tokens, width = x0.shape
+def run_chain(sections, along_y, row_len, rows, segs, wqkv, wout, gain, cot):
+    tokens, width = cot.shape
     head = wout.shape[0]
     chunks = width // CHUNK
-    spread = bg.shape[0] * BLOCK // head
+    each = sections // along_y
+    blocks = head // BLOCK
     vmem = pl.BlockSpec(memory_space=pltpu.VMEM)
     dma = pltpu.SemaphoreType.DMA
     square = (head, tokens)
     return pl.pallas_call(
-        functools.partial(chain_kernel, sections, width, spread),
+        functools.partial(chain_kernel, sections, along_y, row_len),
         out_shape=(
-            jax.ShapeDtypeStruct((chunks, tokens, CHUNK), BF16),
-            jax.ShapeDtypeStruct((chunks, 1, CHUNK), F32),
+            jax.ShapeDtypeStruct((tokens, width), BF16),
+            jax.ShapeDtypeStruct((chunks, CHUNK), F32),
         ),
-        in_specs=[vmem] * 10,
+        in_specs=[vmem] * 6,
         out_specs=(vmem, vmem),
         scratch_shapes=[
+            pltpu.VMEM(rows.shape, BF16),
+            pltpu.VMEM(segs.shape, BF16),
+            pltpu.VMEM((each, PIECES, BLOCK, width // PIECES), BF16),
+            pltpu.VMEM((sections, blocks, BLOCK, 4 * head), BF16),
             pltpu.VMEM((sections, 4 * head, head), BF16),
             pltpu.VMEM((4 * head, tokens), F32),
+            pltpu.VMEM(square, F32),
+            pltpu.VMEM((tokens, tokens), F32),
             pltpu.VMEM((sections, *square), BF16),
             pltpu.VMEM(square, BF16),
             pltpu.VMEM((8, tokens), F32),
@@ -316,65 +532,46 @@
             pltpu.VMEM((tokens, tokens), F32),
             pltpu.VMEM(square, F32),
             pltpu.VMEM((8, tokens), F32),
+            pltpu.VMEM((chunks, CHUNK), F32),
+            pltpu.VMEM((chunks, CHUNK), F32),
+            pltpu.VMEM((ALONG_X, chunks, CHUNK), F32),
+            pltpu.VMEM((along_y, chunks, CHUNK), F32),
+            dma((2,)), dma((2,)), dma((each, PIECES)), dma((each, PIECES)),
+            dma((each, along_y)), dma((sections,)),
+            dma((sections, ALONG_X)), dma((sections, ALONG_X)),
+            dma((sections,)), dma((sections,)),
             dma((sections,)), dma((sections,)), dma, dma,
             dma((sections,)), dma((sections,)), dma, dma,
             dma((chunks,)), dma((chunks,)), dma((chunks,)), dma((chunks,)),
+            dma, dma, dma((ALONG_X,)), dma((ALONG_X,)), dma((along_y,)), dma((along_y,)),
         ],
         compiler_params=pltpu.CompilerParams(
             collective_id=0, has_side_effects=True, vmem_limit_bytes=48 << 20
         ),
-    )(zt0, et, n0, bias, bg, wqkv, wout, gain, x0, cot)
-
-
-def exchanged(array):
-    return lax.all_to_all(array, "group", split_axis=0, concat_axis=0, tiled=True)
+    )(rows, segs, wqkv, wout, gain, cot)
 
 
 def local(tokens_in, cotangent, gains, w_qkv, w_out, segments, plan):
     sections = lax.axis_size("section")
-    plane = lax.axis_size(("dp", "group"))
-    place = lax.axis_index(("dp", "group"))
+    along_y = lax.axis_size("dp") // ALONG_X
+    core = lax.axis_index("group")
     rows_dev = plan.shape[1]
     width = tokens_in.shape[1]
     row_len = segments.shape[1]
-    tokens = rows_dev * row_len
-    gain, wqkv, wout = gains[0], w_qkv[0], w_out[0]
-    head = wout.shape[0]
-    chunks = width // CHUNK
-
-    blocks = head // BLOCK
-    spread = plane // blocks
-    each = sections // spread
-    own_rows = lax.dynamic_slice_in_dim(wout, lax.rem(place, blocks) * BLOCK, BLOCK, 0)
-    all_rows = lax.all_gather(own_rows, "section").reshape(each, spread, BLOCK, width)
-    mine = lax.dynamic_index_in_dim(all_rows, lax.div(place, blocks), 1, keepdims=False)
-    scaled = (wqkv.astype(F32) * gain[:, None]).astype(BF16)
-    both = jnp.concatenate([scaled, wout.T], axis=1)
-    piece = nn(mine.reshape(each * BLOCK, width), both).astype(BF16).reshape(each, BLOCK, 4 * head)
-    bg = lax.all_gather(piece, ("dp", "group"))
-
-    rows = jnp.take(tokens_in.reshape(rows_dev, row_len, width), plan[0], axis=0)
-    segs = jnp.take(segments, plan[0], axis=0).astype(BF16)
-    x0 = exchanged(rows).reshape(tokens, width)
-    seg = exchanged(segs).reshape(tokens)
-
-    zt0 = lax.dot_general(both, x0, (((0,), (1,)), ((), ())), preferred_element_type=F32)
-    et = nt(wout, cotangent)
-    n0 = jnp.broadcast_to(jnp.sum(jnp.square(x0.astype(F32)), axis=1)[None], (8, tokens))
-    at = jnp.arange(tokens)
-    allowed = (
-        (at[:, None] <= at[None, :])
-        & (at[:, None] // row_len == at[None, :] // row_len)
-        & (seg[:, None] == seg[None, :])
+    half = rows_dev // 2 * row_len
+
+    order = plan[0]
+    blocks = tokens_in.reshape(rows_dev, row_len, width)
+    rows = blocks.at[order].get(mode="promise_in_bounds").reshape(2, half, width)
+    segs = segments.at[order].get(mode="promise_in_bounds").astype(BF16).reshape(2, half)
+    spot = jnp.arange(2 * half) // half == core
+    segs = jnp.where(spot[None], jnp.concatenate([segs, segs], axis=1), 0)
+    segs = jnp.broadcast_to(segs[:, None, :], (2, 16, 2 * half))
+
+    grads, gain_whole = run_chain(
+        sections, along_y, row_len, rows, segs, w_qkv[0], w_out[0], gains, cotangent
     )
-    bias = jnp.where(allowed, 0.0, -1e30).astype(F32)
-
-    grads, gsum = run_chain(
-        sections, zt0, et, n0, bias, bg, wqkv, wout, gain.reshape(chunks, 1, CHUNK), x0, cotangent
-    )
-    grads = grads.transpose(1, 0, 2).reshape(1, tokens, width)
-    gain_whole = lax.psum(gsum.reshape(1, width), ("dp", "group"))
-    return grads, gain_whole
+    return grads[None], gain_whole.reshape(1, width)
 
 
 def solution(mesh):

time: 608 us -> 218 us (0.36)
  blocking collectives: 255 us -> 0 us
  waiting for transfers between devices: 145 us -> 0 us
  Pallas kernels: 146 us -> 208 us
  starting transfers between devices: 17 us -> 0 us
  between operations: 14.2 us -> 0.69 us
  matrix products: 8.51 us -> 0 us
    psum x1 -> x0, blocking collectives: 255 us -> none  [local(): gain_whole = lax.psum(gsum.reshape(1, width), ('dp', 'group'))]
    all_gather x2 -> x0, waiting for transfers between devices: 145 us -> none  [the longest x1 72.8 us: local(): lax.all_gather(own_rows, 'section').reshape(each, spread, BLOCK, width)]
    pallas_call x1, Pallas kernels: 146 us -> 208 us  [run_chain(): pl.pallas_call(functools.partial(chain_kernel, sections, along_y, row_len...]
    all_to_all x2 -> x0, starting transfers between devices: 16.9 us -> none  [exchanged(): lax.all_to_all(array, 'group', split_axis=0, concat_axis=0, tiled=True)]
    dot_general x3 -> x0, matrix products: 8.51 us -> none  [the longest x1 3.51 us: local(): lax.dot_general(both, x0, (((0,), (1,)), ((), ())), preferred_element_typ...]
  transfers between devices with their start and end apart: 4 -> 0, of which waited for: 3 -> 0; matrix products, arithmetic and copies ran while one was open for 3% -> 0% of each run, Pallas kernels for 0% -> 0%
where the time goes in v2:
time: 218 us; the launch traced here: 217 us
  Pallas kernels  208 us (95%)
  local copies, waits for them, and re-layouts  7.91 us (4%)
    pallas_call x1, Pallas kernels, run_chain(): pl.pallas_call(functools.partial(chain_kernel, sections, along_y, row_len...  208 us
    unnamed x10, local copies, waits for them, and re-layouts  5.96 us

profile of v2, /device:TPU:1, one launch (start us, length us, event | category | flops | bytes accessed | tf_op | source)
XLA Modules:
  0.0 217.4 jit_solution(13627313495405807569)
XLA Ops:
  0.6 0.0 copy-start
  0.7 1.2 copy-done
  1.9 0.7 fusion.1
  2.5 1.2 gather_fusion.1
  3.8 0.1 convert_element_type.13
  3.9 0.1 broadcast_select_fusion
  4.0 0.6 gather_fusion
  4.6 0.0 copy-start.1
  4.6 1.2 copy-done.1
  5.8 0.0 copy-start.2
  5.8 1.2 copy-done.2
  7.0 0.0 copy-start.3
  7.0 0.7 copy-done.3
  7.7 208.0 %shard_map.86 = (bf16[128,4096]{1,0:T(8,128)(2,1)S(1)}, f32[16,256]{1,0:T(8,128)S(1)}) custom-call(bf16[2,64,4096]{2,1,0:T(8,128)(2,1)S(1)} %bitcast.13, bf16[2,16,128]{2,1,0:T(8,128)(2,1)S(1)} %broadcast_in_dim.26.segs_ref, bf16[4096,384]{1,0:T(8,128)(2,1)} %bitcast.17, bf16[128,4096]{1,0:T(8,128)(2,1)S(1)} %bitcast.15, f32[1,4096]{1,0:T(1,128)S(1)} %copy-done.3, ...), custom_call_target="tpu_custom_call" | custom-call | tf_op jit(solution)/shard_map/pallas_call | solution.py:497
  215.8 0.6 copy.9
  216.4 1.0 copy.11
  (4 shorter events, 0.0 us)
Async XLA Ops:
  0.6 1.2 copy-start
  4.6 1.2 copy-start.1
  5.8 1.2 copy-start.2
  7.0 0.7 copy-start.3

commit v3 on v2

--- a/solution.py
+++ b/solution.py
@@ -11,11 +11,12 @@
 MESH = pl.DeviceIdType.MESH
 F32 = jnp.float32
 BF16 = jnp.bfloat16
-CHUNK = 256
+CHUNK = 128
 BLOCK = 16
 PIECES = 4
 ALONG_X = 4
-AHEAD = 6
+AHEAD = 8
+LAG = 3
 
 
 def nn(a, b):
@@ -31,8 +32,8 @@
     rows_ref, segs_ref, wqkv_ref, wout_ref, gain_ref, cot_ref,
     out_ref, gtotal_ref,
     x0, seg_in, zb, bg, bgt, zt, et, bias, a_in, a_own, n_in, n_out, f_in, f_out, s_in, s_out,
-    x_in, x_out, c_in,
-    mt, m_tok, a_tok, beta_cols,
+    x_in, x_out, c_in, c_out,
+    mt, m_tok, a_tok, sum_cols,
     q_s, k_s, v_s, p_s, y_s, r_s,
     g_own, g_pair, g_x, g_y,
     e_send, e_recv, z_send, z_recv, by_send, by_recv, bx_send, bx_recv, bc_send, bc_recv,
@@ -62,12 +63,20 @@
         return my_y * ALONG_X + lax.rem(my_x + d, ALONG_X)
 
     barrier = pltpu.get_barrier_semaphore()
-    peers = [{"section": up}, {"section": down}, {"group": other}]
+    peers = [{"group": other}]
     peers += [{"dp": y_peer(d)} for d in range(1, along_y)]
     peers += [{"dp": x_peer(d)} for d in range(1, ALONG_X)]
     for peer in peers:
         pl.semaphore_signal(barrier, inc=1, device_id=peer, device_id_type=MESH)
 
+    @pl.when(me < last)
+    def _():
+        pl.semaphore_signal(barrier, inc=1, device_id={"section": up}, device_id_type=MESH)
+
+    @pl.when(me > 0)
+    def _():
+        pl.semaphore_signal(barrier, inc=1, device_id={"section": down}, device_id_type=MESH)
+
     def copy_to(src, dst, ssem, rsem, where):
         return pltpu.make_async_remote_copy(
             src_ref=src, dst_ref=dst, send_sem=ssem, recv_sem=rsem,
@@ -134,7 +143,7 @@
 
     def c_copy(k):
         return copy_to(
-            out_ref.at[:, lanes(k)], c_in.at[k], c_send.at[k], c_recv.at[k], {"section": down}
+            c_out.at[k], c_in.at[k], c_send.at[k], c_recv.at[k], {"section": down}
         )
 
     def gp_copy():
@@ -162,7 +171,8 @@
             for p in range(PIECES):
                 zb[h, p] = wout_ref[pl.ds(start, BLOCK), p * piece : (p + 1) * piece]
 
-    pl.semaphore_wait(barrier, len(peers))
+    along_z = jnp.where(me < last, 1, 0) + jnp.where(me > 0, 1, 0)
+    pl.semaphore_wait(barrier, len(peers) + along_z)
     rows_copy().start()
     segs_copy().start()
     for h in range(each):
@@ -240,31 +250,37 @@
             for d in range(1, along_y):
                 by_copy(h, d).start()
 
-    def over_x(t, carry):
-        @pl.when(lax.rem(t, along_y) != my_y)
-        def _():
-            by_arrival(t).wait_recv()
-
-        for d in range(1, ALONG_X):
-            bx_copy(t, d).start()
-        return carry
-
-    lax.fori_loop(0, me + 1, over_x, 0)
-
-    def over_cores(t, carry):
-        for d in range(1, ALONG_X):
-            bx_copy(t, d).wait_recv()
-        bc_copy(t).start()
-        return carry
-
-    lax.fori_loop(0, me + 1, over_cores, 0)
-
-    def turn(t, carry):
-        bc_copy(t).wait_recv()
-        bgt[t] = block_of(t).T
-        return carry
-
-    lax.fori_loop(0, me + 1, turn, 0)
+        top = jnp.minimum(me, along_y * h + along_y - 1)
+        count = jnp.maximum(top - along_y * h + 1, 0)
+
+        def flow(i, carry):
+            @pl.when(i < count)
+            def _():
+                t = top - i
+
+                @pl.when(lax.rem(t, along_y) != my_y)
+                def _():
+                    by_arrival(t).wait_recv()
+
+                for d in range(1, ALONG_X):
+                    bx_copy(t, d).start()
+
+            @pl.when((i >= LAG) & (i < count + LAG))
+            def _():
+                t = top - (i - LAG)
+                for d in range(1, ALONG_X):
+                    bx_copy(t, d).wait_recv()
+                bc_copy(t).start()
+
+            @pl.when(i >= 2 * LAG)
+            def _():
+                t = top - (i - 2 * LAG)
+                bc_copy(t).wait_recv()
+                bgt[t] = block_of(t).T
+
+            return carry
+
+        lax.fori_loop(0, jnp.where(count > 0, count + 2 * LAG, 0), flow, 0)
 
     def gather(t, carry):
         a_relay(t).wait_recv()
@@ -379,53 +395,86 @@
 
     lax.fori_loop(0, me, f_step, 0)
 
-    lax.fori_loop(pause, chunks, x_step, 0)
-
-    m_tok[:, 0:head] = mt[0:head, :].astype(F32).T.astype(BF16)
-    m_tok[:, head : 2 * head] = mt[head : 2 * head, :].astype(F32).T.astype(BF16)
-    m_tok[:, 2 * head :] = mt[2 * head : 3 * head, :].astype(F32).T.astype(BF16)
-    beta_cols[...] = jnp.broadcast_to(beta, (tokens, tokens)).T
+    for i in range(4):
+        part = slice(i * head, (i + 1) * head)
+        m_tok[:, part] = mt[part, :].astype(F32).T.astype(BF16)
+    sum_cols[...] = jnp.broadcast_to(summed + beta, (tokens, tokens)).T
+
+    def turned(k):
+        start = pl.multiple_of(k * wide, wide)
+        return nt(m_tok[:, 0 : 3 * head], wqkv_ref[pl.ds(start, wide), :])
+
+    def gain_step(k, carry):
+        g_own[pl.ds(k, 1), :] = jnp.sum(x_in[k].astype(F32) * turned(k), axis=0, keepdims=True)
+        return carry
+
+    def gains_0():
+        lax.fori_loop(0, chunks, gain_step, 0)
+        gp_copy().start()
+
+    def gains_1():
+        gp_copy().wait_recv()
+        g_x[my_x] = g_own[...] + g_pair[...]
+        for d in range(1, ALONG_X):
+            gx_copy(d).start()
+
+    def gains_2():
+        for d in range(1, ALONG_X):
+            gx_copy(d).wait_recv()
+        total = g_x[0]
+        for i in range(1, ALONG_X):
+            total += g_x[i]
+        g_y[my_y] = total
+        for d in range(1, along_y):
+            gy_copy(d).start()
+
+    def gains_3():
+        for d in range(1, along_y):
+            gy_copy(d).wait_recv()
+        total = g_y[0]
+        for i in range(1, along_y):
+            total += g_y[i]
+        gtotal_ref[...] = total
 
     def c_step(k, carry):
         @pl.when(me < last)
         def _():
             c_copy(k).wait_recv()
 
-        start = pl.multiple_of(k * wide, wide)
-        turned = nt(m_tok[...], wqkv_ref[pl.ds(start, wide), :])
-        x = x_in[k].astype(F32)
-        fall = jnp.concatenate([beta_cols[...]] * (wide // tokens), axis=1)
-        grad = c_in[k].astype(F32) + gain_ref[0:1, lanes(k)] * turned - fall * x
-        g_own[pl.ds(k, 1), :] = jnp.sum(x * turned, axis=0, keepdims=True)
-        out_ref[:, lanes(k)] = grad.astype(BF16)
+        fresh = c_in[k].astype(F32) + gain_ref[0:1, lanes(k)] * turned(k)
+        fresh += nn(m_tok[:, 3 * head :], wout_ref[:, lanes(k)])
 
         @pl.when(me > 0)
         def _():
+            c_out[k] = fresh.astype(BF16)
             c_copy(k).start()
 
+        @pl.when(me == 0)
+        def _():
+            out_ref[:, lanes(k)] = (fresh - sum_cols[...] * x_in[k].astype(F32)).astype(BF16)
+
         return carry
 
-    lax.fori_loop(0, chunks, c_step, 0)
-
-    gp_copy().start()
-    gp_copy().wait_recv()
-    g_x[my_x] = g_own[...] + g_pair[...]
-    for d in range(1, ALONG_X):
-        gx_copy(d).start()
-    for d in range(1, ALONG_X):
-        gx_copy(d).wait_recv()
-    total = g_x[0]
-    for i in range(1, ALONG_X):
-        total += g_x[i]
-    g_y[my_y] = total
-    for d in range(1, along_y):
-        gy_copy(d).start()
-    for d in range(1, along_y):
-        gy_copy(d).wait_recv()
-    total = g_y[0]
-    for i in range(1, along_y):
-        total += g_y[i]
-    gtotal_ref[...] = total
+    def rest_step(k, carry):
+        rest = c_out[k].astype(F32) - sum_cols[...] * x_in[k].astype(F32)
+        out_ref[:, lanes(k)] = rest.astype(BF16)
+        return carry
+
+    stages = (gains_0, gains_1, gains_2, gains_3)
+    for i, stage in enumerate(stages):
+        pl.when(me == 0)(stage)
+        if i < 3:
+            lax.fori_loop(i * chunks // 3, (i + 1) * chunks // 3, c_step, 0)
+
+    lax.fori_loop(pause, chunks, x_step, 0)
+
+    @pl.when(me > 0)
+    def _():
+        gains_0()
+        lax.fori_loop(0, chunks, rest_step, 0)
+        gains_1()
+        gains_2()
+        gains_3()
 
     rows_copy().wait_send()
     segs_copy().wait_send()
@@ -522,8 +571,9 @@
             pltpu.VMEM((chunks, tokens, CHUNK), BF16),
             pltpu.VMEM((chunks, tokens, CHUNK), BF16),
             pltpu.VMEM((chunks, tokens, CHUNK), BF16),
+            pltpu.VMEM((chunks, tokens, CHUNK), BF16),
             pltpu.VMEM((4 * head, tokens), BF16),
-            pltpu.VMEM((tokens, 3 * head), BF16),
+            pltpu.VMEM((tokens, 4 * head), BF16),
             pltpu.VMEM((tokens, head), BF16),
             pltpu.VMEM((tokens, tokens), F32),
             pltpu.VMEM(square, F32),

time: 218 us -> 188 us (0.86)
  the two profiles are of different devices: /device:TPU:1 before, /device:TPU:64 now
where the time goes in v3:
time: 188 us
  Pallas kernels  179 us (95%)
  local copies, waits for them, and re-layouts  7.89 us (4%)
    pallas_call x1, Pallas kernels, run_chain(): pl.pallas_call(functools.partial(chain_kernel, sections, along_y, row_len...  179 us
    unnamed x10, local copies, waits for them, and re-layouts  5.94 us

profile of v3, /device:TPU:64, one launch (start us, length us, event | category | flops | bytes accessed | tf_op | source)
XLA Modules:
  0.0 188.1 jit_solution(16118080260330335916)
XLA Ops:
  0.6 0.0 copy-start
  0.7 1.2 copy-done
  1.9 0.7 fusion.1
  2.5 1.2 gather_fusion.1
  3.8 0.1 convert_element_type.13
  3.9 0.1 broadcast_select_fusion
  4.0 0.6 gather_fusion
  4.6 0.0 copy-start.1
  4.6 1.2 copy-done.1
  5.8 0.0 copy-start.2
  5.8 1.2 copy-done.2
  7.0 0.0 copy-start.3
  7.0 0.7 copy-done.3
  7.7 178.8 %shard_map.86 = (bf16[128,4096]{1,0:T(8,128)(2,1)S(1)}, f32[32,128]{1,0:T(8,128)S(1)}) custom-call(bf16[2,64,4096]{2,1,0:T(8,128)(2,1)S(1)} %bitcast.11, bf16[2,16,128]{2,1,0:T(8,128)(2,1)S(1)} %broadcast_in_dim.26.segs_ref, bf16[4096,384]{1,0:T(8,128)(2,1)} %bitcast.15, bf16[128,4096]{1,0:T(8,128)(2,1)S(1)} %bitcast.13, f32[1,4096]{1,0:T(1,128)S(1)} %copy-done.3, ...), custom_call_target="tpu_custom_call" | custom-call | tf_op jit(solution)/shard_map/pallas_call | solution.py:546
  186.5 1.0 copy.11
  187.5 0.6 copy.12
  (4 shorter events, 0.0 us)
Async XLA Ops:
  0.6 1.2 copy-start
  4.6 1.2 copy-start.1
  5.8 1.2 copy-start.2
  7.0 0.7 copy-start.3

commit v4 on v3

--- a/solution.py
+++ b/solution.py
@@ -29,9 +29,9 @@
 
 def chain_kernel(
     sections, along_y, row_len,
-    rows_ref, segs_ref, wqkv_ref, wout_ref, gain_ref, cot_ref,
-    out_ref, gtotal_ref,
-    x0, seg_in, zb, bg, bgt, zt, et, bias, a_in, a_own, n_in, n_out, f_in, f_out, s_in, s_out,
+    rows_ref, segs_ref, wqkv_hbm, wout_hbm, gain_hbm, cot_hbm,
+    out_hbm, gtotal_ref,
+    wqkv_ref, wout_ref, gain_ref, cot_ref, out_ref, x0, seg_in, zb, bg, bgt, zt, et, bias, a_in, a_own, n_in, n_out, f_in, f_out, s_in, s_out,
     x_in, x_out, c_in, c_out,
     mt, m_tok, a_tok, sum_cols,
     q_s, k_s, v_s, p_s, y_s, r_s,
@@ -40,6 +40,7 @@
     a_send, a_recv, n_send, n_recv, f_send, f_recv, s_send, s_recv,
     x_send, x_recv, c_send, c_recv,
     gp_send, gp_recv, gx_send, gx_recv, gy_send, gy_recv,
+    in_sem, out_sem, pair_sem,
 ):
     me = lax.axis_index("section")
     place = lax.axis_index("dp")
@@ -62,6 +63,18 @@
     def x_peer(d):
         return my_y * ALONG_X + lax.rem(my_x + d, ALONG_X)
 
+    loads = [
+        pltpu.make_async_copy(src, dst, in_sem.at[i])
+        for i, (src, dst) in enumerate(
+            [
+                (wout_hbm, wout_ref), (cot_hbm, cot_ref), (gain_hbm, gain_ref),
+                (wqkv_hbm, wqkv_ref),
+            ]
+        )
+    ]
+    for load in loads:
+        load.start()
+
     barrier = pltpu.get_barrier_semaphore()
     peers = [{"group": other}]
     peers += [{"dp": y_peer(d)} for d in range(1, along_y)]
@@ -162,7 +175,17 @@
     def block_of(t):
         return bg[t].reshape(head, 4 * head)
 
+    def o_copy(k):
+        part = lanes(k)
+        return pltpu.make_async_copy(out_ref.at[:, part], out_hbm.at[:, part], out_sem.at[k])
+
+    def tell_pair(i):
+        pl.semaphore_signal(
+            pair_sem.at[i], inc=1, device_id={"group": other}, device_id_type=MESH
+        )
+
     piece = width // PIECES
+    loads[0].wait()
     for h in range(each):
 
         @pl.when(me == my_y + along_y * h)
@@ -184,6 +207,7 @@
 
     x0[core] = rows_ref[core]
     seg_in[core] = segs_ref[core]
+    loads[1].wait()
     et[...] = nt(wout_ref[...], cot_ref[...])
 
     @pl.when(me == last)
@@ -193,6 +217,8 @@
         s_in[...] = jnp.zeros_like(s_in)
         f_in[last] = jnp.zeros_like(f_in[last])
 
+    loads[2].wait()
+    loads[3].wait()
     rows_copy().wait_recv()
     segs_copy().wait_recv()
 
@@ -325,6 +351,7 @@
     def _():
         n_copy().start()
 
+    tell_pair(0)
     q_s[...] = qt
     k_s[...] = kt
     v_s[...] = vt
@@ -332,6 +359,8 @@
     y_s[...] = y1
     r_s[...] = jnp.broadcast_to(scale_r, r_s.shape)
     a_tok[...] = at.astype(F32).T.astype(BF16)
+
+    pl.semaphore_wait(pair_sem.at[0], 1)
 
     def x_step(k, carry):
         @pl.when(me > 0)
@@ -387,13 +416,17 @@
         f_out[t] = (f_in[t].astype(F32) + nn(block_of(t), mt[...])).astype(BF16)
         f_copy(t).start()
 
-        @pl.when(i == 0)
-        def _():
-            s_copy().start()
-
         return carry
 
-    lax.fori_loop(0, me, f_step, 0)
+    lax.fori_loop(0, jnp.minimum(me, 1), f_step, 0)
+
+    @pl.when(me > 0)
+    def _():
+        s_copy().start()
+
+    tell_pair(1)
+    pl.semaphore_wait(pair_sem.at[1], 1)
+    lax.fori_loop(1, me, f_step, 0)
 
     for i in range(4):
         part = slice(i * head, (i + 1) * head)
@@ -404,12 +437,21 @@
         start = pl.multiple_of(k * wide, wide)
         return nt(m_tok[:, 0 : 3 * head], wqkv_ref[pl.ds(start, wide), :])
 
+    def gain_of(k, value):
+        g_own[pl.ds(k, 1), :] = jnp.sum(x_in[k].astype(F32) * value, axis=0, keepdims=True)
+
     def gain_step(k, carry):
-        g_own[pl.ds(k, 1), :] = jnp.sum(x_in[k].astype(F32) * turned(k), axis=0, keepdims=True)
+        gain_of(k, turned(k))
         return carry
 
+    def finish(k, value):
+        out_ref[:, lanes(k)] = (value - sum_cols[...] * x_in[k].astype(F32)).astype(BF16)
+        o_copy(k).start()
+
+    late = last - chunks // AHEAD + 1
+
     def gains_0():
-        lax.fori_loop(0, chunks, gain_step, 0)
+        lax.fori_loop(0, jnp.where((me == 0) | (me >= late), chunks, 0), gain_step, 0)
         gp_copy().start()
 
     def gains_1():
@@ -441,7 +483,8 @@
         def _():
             c_copy(k).wait_recv()
 
-        fresh = c_in[k].astype(F32) + gain_ref[0:1, lanes(k)] * turned(k)
+        value = turned(k)
+        fresh = c_in[k].astype(F32) + gain_ref[0:1, lanes(k)] * value
         fresh += nn(m_tok[:, 3 * head :], wout_ref[:, lanes(k)])
 
         @pl.when(me > 0)
@@ -449,15 +492,18 @@
             c_out[k] = fresh.astype(BF16)
             c_copy(k).start()
 
-        @pl.when(me == 0)
-        def _():
-            out_ref[:, lanes(k)] = (fresh - sum_cols[...] * x_in[k].astype(F32)).astype(BF16)
+        @pl.when(me < late)
+        def _():
+            finish(k, fresh)
+
+        @pl.when((me > 0) & (me < late))
+        def _():
+            gain_of(k, value)
 
         return carry
 
     def rest_step(k, carry):
-        rest = c_out[k].astype(F32) - sum_cols[...] * x_in[k].astype(F32)
-        out_ref[:, lanes(k)] = rest.astype(BF16)
+        finish(k, c_out[k].astype(F32))
         return carry
 
     stages = (gains_0, gains_1, gains_2, gains_3)
@@ -471,11 +517,16 @@
     @pl.when(me > 0)
     def _():
         gains_0()
-        lax.fori_loop(0, chunks, rest_step, 0)
+        lax.fori_loop(0, jnp.where(me >= late, chunks, 0), rest_step, 0)
         gains_1()
         gains_2()
         gains_3()
 
+    def done_o(k, carry):
+        o_copy(k).wait()
+        return carry
+
+    lax.fori_loop(0, chunks, done_o, 0)
     rows_copy().wait_send()
     segs_copy().wait_send()
     gp_copy().wait_send()
@@ -541,6 +592,7 @@
     each = sections // along_y
     blocks = head // BLOCK
     vmem = pl.BlockSpec(memory_space=pltpu.VMEM)
+    anywhere = pl.BlockSpec(memory_space=pl.ANY)
     dma = pltpu.SemaphoreType.DMA
     square = (head, tokens)
     return pl.pallas_call(
@@ -549,9 +601,14 @@
             jax.ShapeDtypeStruct((tokens, width), BF16),
             jax.ShapeDtypeStruct((chunks, CHUNK), F32),
         ),
-        in_specs=[vmem] * 6,
-        out_specs=(vmem, vmem),
+        in_specs=[vmem] * 2 + [anywhere] * 4,
+        out_specs=(anywhere, vmem),
         scratch_shapes=[
+            pltpu.VMEM(wqkv.shape, BF16),
+            pltpu.VMEM(wout.shape, BF16),
+            pltpu.VMEM(gain.shape, F32),
+            pltpu.VMEM(cot.shape, BF16),
+            pltpu.VMEM(cot.shape, BF16),
             pltpu.VMEM(rows.shape, BF16),
             pltpu.VMEM(segs.shape, BF16),
             pltpu.VMEM((each, PIECES, BLOCK, width // PIECES), BF16),
@@ -594,6 +651,7 @@
             dma((sections,)), dma((sections,)), dma, dma,
             dma((chunks,)), dma((chunks,)), dma((chunks,)), dma((chunks,)),
             dma, dma, dma((ALONG_X,)), dma((ALONG_X,)), dma((along_y,)), dma((along_y,)),
+            dma((4,)), dma((chunks,)), pltpu.SemaphoreType.REGULAR((2,)),
         ],
         compiler_params=pltpu.CompilerParams(
             collective_id=0, has_side_effects=True, vmem_limit_bytes=48 << 20

time: 188 us -> 194 us (1.032)
  Pallas kernels: 179 us -> 184 us
    pallas_call x1, Pallas kernels: 179 us -> 184 us  [run_chain(): pl.pallas_call(functools.partial(chain_kernel, sections, along_y, row_len...]
where the time goes in v4:
time: 194 us; the launch traced here: 193 us
  Pallas kernels  184 us (95%)
  local copies, waits for them, and re-layouts  7.89 us (4%)
    pallas_call x1, Pallas kernels, run_chain(): pl.pallas_call(functools.partial(chain_kernel, sections, along_y, row_len...  184 us
    unnamed x10, local copies, waits for them, and re-layouts  5.94 us

profile of v4, /device:TPU:64, one launch (start us, length us, event | category | flops | bytes accessed | tf_op | source)
XLA Modules:
  0.0 193.4 jit_solution(14172248486595593462)
XLA Ops:
  0.6 0.0 copy-start
  0.7 1.2 copy-done
  1.9 0.7 fusion.1
  2.5 1.2 gather_fusion.1
  3.8 0.1 convert_element_type.13
  3.9 0.1 broadcast_select_fusion
  4.0 0.6 gather_fusion
  4.6 0.0 copy-start.1
  4.6 1.2 copy-done.1
  5.8 0.0 copy-start.2
  5.8 1.2 copy-done.2
  7.0 0.0 copy-start.3
  7.0 0.7 copy-done.3
  7.7 184.1 %shard_map.86 = (bf16[128,4096]{1,0:T(8,128)(2,1)S(1)}, f32[32,128]{1,0:T(8,128)S(1)}) custom-call(bf16[2,64,4096]{2,1,0:T(8,128)(2,1)S(1)} %bitcast.11, bf16[2,16,128]{2,1,0:T(8,128)(2,1)S(1)} %broadcast_in_dim.26.segs_ref, bf16[4096,384]{1,0:T(8,128)(2,1)} %bitcast.15, bf16[128,4096]{1,0:T(8,128)(2,1)S(1)} %bitcast.13, f32[1,4096]{1,0:T(1,128)S(1)} %copy-done.3, ...), custom_call_target="tpu_custom_call" | custom-call | tf_op jit(solution)/shard_map/pallas_call | solution.py:598
  191.9 1.0 copy.11
  192.8 0.6 copy.12
  (4 shorter events, 0.0 us)
Async XLA Ops:
  0.6 1.2 copy-start
  4.6 1.2 copy-start.1
  5.8 1.2 copy-start.2
  7.0 0.7 copy-start.3

commit v5 on v4

--- a/solution.py
+++ b/solution.py
@@ -351,7 +351,6 @@
     def _():
         n_copy().start()
 
-    tell_pair(0)
     q_s[...] = qt
     k_s[...] = kt
     v_s[...] = vt
@@ -359,8 +358,6 @@
     y_s[...] = y1
     r_s[...] = jnp.broadcast_to(scale_r, r_s.shape)
     a_tok[...] = at.astype(F32).T.astype(BF16)
-
-    pl.semaphore_wait(pair_sem.at[0], 1)
 
     def x_step(k, carry):
         @pl.when(me > 0)
@@ -424,8 +421,6 @@
     def _():
         s_copy().start()
 
-    tell_pair(1)
-    pl.semaphore_wait(pair_sem.at[1], 1)
     lax.fori_loop(1, me, f_step, 0)
 
     for i in range(4):

time: 194 us -> 181 us (0.933)
  the two profiles are of different devices: /device:TPU:64 before, /device:TPU:1 now
where the time goes in v5:
time: 181 us; the launch traced here: 179 us
  Pallas kernels  170 us (94%)
  local copies, waits for them, and re-layouts  7.89 us (4%)
    pallas_call x1, Pallas kernels, run_chain(): pl.pallas_call(functools.partial(chain_kernel, sections, along_y, row_len...  170 us
    unnamed x10, local copies, waits for them, and re-layouts  5.94 us

profile of v5, /device:TPU:1, one launch (start us, length us, event | category | flops | bytes accessed | tf_op | source)
XLA Modules:
  0.0 179.3 jit_solution(5179226111636901638)
XLA Ops:
  0.6 0.0 copy-start
  0.7 1.2 copy-done
  1.9 0.7 fusion.1
  2.5 1.2 gather_fusion.1
  3.8 0.1 convert_element_type.13
  3.9 0.1 broadcast_select_fusion
  4.0 0.6 gather_fusion
  4.6 0.0 copy-start.1
  4.6 1.2 copy-done.1
  5.8 0.0 copy-start.2
  5.8 1.2 copy-done.2
  7.0 0.0 copy-start.3
  7.0 0.7 copy-done.3
  7.7 170.0 %shard_map.86 = (bf16[128,4096]{1,0:T(8,128)(2,1)S(1)}, f32[32,128]{1,0:T(8,128)S(1)}) custom-call(bf16[2,64,4096]{2,1,0:T(8,128)(2,1)S(1)} %bitcast.11, bf16[2,16,128]{2,1,0:T(8,128)(2,1)S(1)} %broadcast_in_dim.26.segs_ref, bf16[4096,384]{1,0:T(8,128)(2,1)} %bitcast.15, bf16[128,4096]{1,0:T(8,128)(2,1)S(1)} %bitcast.13, f32[1,4096]{1,0:T(1,128)S(1)} %copy-done.3, ...), custom_call_target="tpu_custom_call" | custom-call | tf_op jit(solution)/shard_map/pallas_call | solution.py:593
  177.7 1.0 copy.11
  178.7 0.6 copy.12
  (4 shorter events, 0.0 us)
Async XLA Ops:
  0.6 1.2 copy-start
  4.6 1.2 copy-start.1
  5.8 1.2 copy-start.2
  7.0 0.7 copy-start.3
